TPU v7x, 32 devices: a whole 2x2x4 slice. The times are simulated.
32 devices in a mesh: section: 8 (over y, x, core), expert: 4 (over z).
Axes of the slice: x: 2, y: 2, z: 4, core: 2. Of those that a mesh axis runs over, the one named last changes fastest.
Arguments:
- acts: bfloat16 [8, 128, 2560], P('section', 'expert'), may hold values from -6 to 6
- incoming: bfloat16 [1, 128, 2560], P(None, 'expert'), may hold values from -6 to 6
- routes: int32 [2, 8, 128, 2], P(None, 'section', 'expert'), may hold values from 0 to 3, all different within a row; in each aligned block of 32 rows (0 to 31, 32 to 63, ..., all dimensions but the last counted through in order) at most 24 rows name the same one
- route_weight: float32 [2, 8, 128, 2], P(None, 'section', 'expert'), may hold values from 0.25 to 1
- norm_gain: float32 [8, 2560], P('section'), may hold values from 0.25 to 1.75
- w_gate: bfloat16 [8, 2560, 3072], P('section', None, 'expert'), may hold values from -0.125 to 0.125
- w_up: bfloat16 [8, 2560, 3072], P('section', None, 'expert'), may hold values from -0.125 to 0.125
- w_down: bfloat16 [8, 3072, 2560], P('section', 'expert'), may hold values from -0.21875 to 0.21875
Outputs:
- section_outputs: bfloat16 [2, 8, 128, 2560], P(None, 'section', 'expert')
Inputs may be any that keep to these rules, and one draw needn't show every extreme that they name: `routes`: a token's 2 experts are distinct; in each aligned block of 32 tokens (the tokens of one device) no expert is chosen more than 24 times, and that count is reached.
All inputs are finite; a program needn't handle non-finite values.
Results may differ from a plain program's by a relative error of at most 0.009.
Values may be sent and summed in bfloat16 or wider, within the bound.
A program may use at most 64 MiB of HBM per device.

v0:
```python
import functools

import jax
import jax.numpy as jnp
from jax import lax
from jax.experimental import pallas as pl
from jax.experimental.pallas import tpu as pltpu
from jax.sharding import PartitionSpec as P

MESH = pl.DeviceIdType.MESH
EXPERTS = 4
CHUNKS = 4
PIECES = 1
RIGHT, LEFT = 0, 1


def kernel(
    n,
    sections,
    acts,
    incoming,
    routes,
    route_weight,
    gain,
    w_gate_hbm,
    w_up_hbm,
    w_down_hbm,
    out,
    w_gate,
    w_up,
    w_down,
    xbuf,
    mixbuf,
    rsin,
    rsout,
    held,
    moved,
    w_sem,
    own_sem,
    inc_sem,
    ag_send,
    ag_recv,
    mix_send,
    mix_recv,
    rs_send,
    rs_recv,
    move_send,
    move_recv,
):
    s = lax.axis_index("section")
    e = lax.axis_index("expert")
    ticks, _, chunks, tokens, cols = xbuf.shape
    group = n // EXPERTS
    width = chunks * cols
    has_right = e < n - 1
    has_left = e > 0
    has_next = s < sections - 1
    has_prev = s > 0
    right = (s, jnp.minimum(e + 1, n - 1))
    left = (s, jnp.maximum(e - 1, 0))
    following = (jnp.minimum(s + 1, sections - 1), e)
    previous = (jnp.maximum(s - 1, 0), e)
    has = (has_right, has_left)
    peer = (right, left)

    weight_copies = []
    for i, (src, dst) in enumerate(
        ((w_gate_hbm, w_gate), (w_up_hbm, w_up), (w_down_hbm, w_down))
    ):
        deep = src.shape[0] // PIECES
        weight_copies.append(
            [
                pltpu.make_async_copy(
                    src.at[pl.ds(p * deep, deep)], dst.at[pl.ds(p * deep, deep)], w_sem.at[i, p]
                )
                for p in range(PIECES)
            ]
        )

    def own_copy(c):
        return pltpu.make_async_copy(
            acts.at[:, pl.ds(c * cols, cols)], xbuf.at[0, e, c], own_sem.at[c]
        )

    def inc_copy(t, c):
        return pltpu.make_async_copy(
            incoming.at[t - 1, :, pl.ds(c * cols, cols)], xbuf.at[t, e, c], inc_sem.at[t, c]
        )

    def ag_copy(way, t, j, c):
        return pltpu.make_async_remote_copy(
            xbuf.at[t, j, c],
            xbuf.at[t, j, c],
            ag_send.at[way, t, j, c],
            ag_recv.at[way, t, j, c],
            device_id=peer[way],
            device_id_type=MESH,
        )

    def mix_copy(way, j):
        return pltpu.make_async_remote_copy(
            mixbuf.at[j],
            mixbuf.at[j],
            mix_send.at[way, j],
            mix_recv.at[way, j],
            device_id=peer[way],
            device_id_type=MESH,
        )

    def rs_copy(way, t, j, c):
        return pltpu.make_async_remote_copy(
            rsout.at[t, j, c],
            rsin.at[way, t, j, c],
            rs_send.at[way, t, j, c],
            rs_recv.at[way, t, j, c],
            device_id=peer[way],
            device_id_type=MESH,
        )

    def move_copy(t, c):
        return pltpu.make_async_remote_copy(
            moved.at[t, c],
            xbuf.at[t + 1, e, c],
            move_send.at[t, c],
            move_recv.at[t, c],
            device_id=following,
            device_id_type=MESH,
        )

    for c in range(chunks):
        own_copy(c).start()

    barrier = pltpu.get_barrier_semaphore()
    around = (
        (has_right, right),
        (has_left, left),
        (has_next, following),
        (has_prev, previous),
    )
    for there, device in around:

        @pl.when(there)
        def _():
            pl.semaphore_signal(barrier, inc=1, device_id=device, device_id_type=MESH)

    for copies in weight_copies:
        for copy in copies:
            copy.start()

    @pl.when(jnp.logical_not(has_prev))
    def _():
        for t in range(1, ticks):
            for c in range(chunks):
                inc_copy(t, c).start()

    lanes = mixbuf.shape[2]
    mixbuf[e] = jnp.zeros_like(mixbuf[e])
    for t in range(ticks):
        chosen = routes[t, 0]
        chosen_weight = route_weight[t, 0]
        for x in range(EXPERTS):
            mixbuf[e, t * EXPERTS + x : t * EXPERTS + x + 1, 0:tokens] = jnp.sum(
                jnp.where(chosen == x, chosen_weight, 0.0), axis=0, keepdims=True
            )

    pl.semaphore_wait(barrier, sum(jnp.where(there, 1, 0) for there, _ in around))

    def send_own(t, c):
        for way in (RIGHT, LEFT):

            @pl.when(has[way])
            def _():
                ag_copy(way, t, e, c).start()

    def partial_of(t, blocks, first):
        scales = []
        for j in blocks:
            squares = jnp.zeros((tokens, 1), jnp.float32)
            for c in range(chunks):
                piece = xbuf[t, j, c].astype(jnp.float32)
                squares = squares + jnp.sum(piece * piece, axis=1, keepdims=True)
            scales.append(lax.rsqrt(squares * (1.0 / width) + 1e-06))

        @pl.when(first)
        def _():
            for copy in weight_copies[0] + weight_copies[1]:
                copy.wait()

        gate_val = up_val = None
        for c in range(chunks):
            span = pl.ds(c * cols, cols)
            normed = jnp.concatenate(
                [
                    (xbuf[t, j, c].astype(jnp.float32) * scale * gain[:, span]).astype(jnp.bfloat16)
                    for j, scale in zip(blocks, scales)
                ],
                axis=0,
            )
            gate_part = jnp.dot(normed, w_gate[span, :], preferred_element_type=jnp.float32)
            up_part = jnp.dot(normed, w_up[span, :], preferred_element_type=jnp.float32)
            gate_val = gate_part if gate_val is None else gate_val + gate_part
            up_val = up_part if up_val is None else up_val + up_part
        hidden = (jax.nn.silu(gate_val) * up_val).astype(jnp.bfloat16)
        expert = e // group
        pick = lax.broadcasted_iota(jnp.int32, (tokens, lanes), 0) == lax.broadcasted_iota(
            jnp.int32, (tokens, lanes), 1
        )
        mixing = [
            jnp.sum(
                jnp.where(pick, mixbuf[j, pl.ds(t * EXPERTS + expert, 1), :], 0.0),
                axis=1,
                keepdims=True,
            )
            for j in blocks
        ]

        @pl.when(first)
        def _():
            for copy in weight_copies[2]:
                copy.wait()

        for c in range(chunks):
            span = pl.ds(c * cols, cols)
            values = jnp.dot(hidden, w_down[:, span], preferred_element_type=jnp.float32)
            for i, j in enumerate(blocks):
                value = values[i * tokens : (i + 1) * tokens] * mixing[i]
                held[j, c] = value
                if len(blocks) > 1:
                    continue
                for way, send in (
                    (RIGHT, jnp.logical_and(jnp.logical_not(has_left), j > e)),
                    (LEFT, jnp.logical_and(jnp.logical_not(has_right), j < e)),
                ):

                    @pl.when(send)
                    def _():
                        rsout[t, j, c] = value.astype(jnp.bfloat16)
                        rs_copy(way, t, j, c).start()

    def tick(t, _):
        for c in range(chunks):

            @pl.when(t == 0)
            def _():
                own_copy(c).wait()

            @pl.when(jnp.logical_and(t > 0, has_prev))
            def _():
                move_copy(jnp.maximum(t - 1, 0), c).wait_recv()

            @pl.when(jnp.logical_and(t > 0, jnp.logical_not(has_prev)))
            def _():
                inc_copy(jnp.maximum(t, 1), c).wait()

            send_own(t, c)

        @pl.when(t == 0)
        def _():
            for way in (RIGHT, LEFT):

                @pl.when(has[way])
                def _():
                    mix_copy(way, e).start()

        def arrive(k):
            for c in range(chunks):
                for way, j in ((RIGHT, e - k), (LEFT, e + k)):

                    @pl.when(jnp.logical_and(j >= 0, j < n))
                    def _():
                        ag_copy(way, t, j, c).wait_recv()

                        @pl.when(has[way])
                        def _():
                            ag_copy(way, t, j, c).start()

                        if c == 0:

                            @pl.when(t == 0)
                            def _():
                                mix_copy(way, j).wait_recv()

                                @pl.when(has[way])
                                def _():
                                    mix_copy(way, j).start()

        def step(i, _):
            k = jnp.where(t == 0, lax.rem(i + 1, n), i)
            there_left, there_right = e - k >= 0, e + k < n

            @pl.when(k > 0)
            def _():
                arrive(k)

            both = jnp.logical_and(k > 0, jnp.logical_and(there_left, there_right))
            first = jnp.logical_and(t == 0, i == 0)

            @pl.when(both)
            def _():
                partial_of(t, (e - k, e + k), first)

            @pl.when(jnp.logical_and(jnp.logical_not(both), jnp.logical_or(there_left, there_right)))
            def _():
                partial_of(t, (jnp.where(there_left, e - k, e + k),), first)

            return 0

        lax.fori_loop(0, n, step, 0)

        from_right, from_left = 2 * (n - 1 - e), 2 * e
        last = jnp.maximum(from_right, from_left)

        def combine(time, _):
            for c in range(chunks):
                for way, there, k, j in (
                    (LEFT, has_right, time - from_right, e - (time - from_right)),
                    (RIGHT, has_left, time - from_left, e + (time - from_left)),
                ):

                    @pl.when(
                        jnp.logical_and(
                            there, jnp.logical_and(k >= 0, jnp.logical_and(j >= 0, j < n))
                        )
                    )
                    def _():
                        rs_copy(way, t, j, c).wait_recv()
                        total = held[j, c] + rsin[way, t, j, c].astype(jnp.float32)

                        @pl.when(k == 0)
                        def _():
                            held[j, c] = total

                        @pl.when(k > 0)
                        def _():
                            rsout[t, j, c] = total.astype(jnp.bfloat16)
                            rs_copy(way, t, j, c).start()

                @pl.when(time == last)
                def _():
                    layer = (xbuf[t, e, c].astype(jnp.float32) + held[e, c]).astype(jnp.bfloat16)
                    out[t, :, pl.ds(c * cols, cols)] = layer

                    @pl.when(jnp.logical_and(t < ticks - 1, has_next))
                    def _():
                        moved[jnp.minimum(t, ticks - 2), c] = layer
                        move_copy(jnp.minimum(t, ticks - 2), c).start()

            return 0

        lax.fori_loop(0, 3 * (n - 1) + 1, combine, 0)
        return 0

    lax.fori_loop(0, ticks, tick, 0)

    def drain(j, _):
        for way, within in (
            (RIGHT, jnp.logical_and(has_right, j <= e)),
            (LEFT, jnp.logical_and(has_left, j >= e)),
        ):

            @pl.when(within)
            def _():
                mix_copy(way, j).wait_send()
                for t in range(ticks):
                    for c in range(chunks):
                        ag_copy(way, t, j, c).wait_send()

        for way, within in ((RIGHT, j > e), (LEFT, j < e)):

            @pl.when(within)
            def _():
                for t in range(ticks):
                    for c in range(chunks):
                        rs_copy(way, t, j, c).wait_send()

        return 0

    lax.fori_loop(0, n, drain, 0)

    @pl.when(has_next)
    def _():
        for t in range(ticks - 1):
            for c in range(chunks):
                move_copy(t, c).wait_send()


def solution(mesh):
    n = mesh.shape["expert"]
    sections = mesh.shape["section"]

    def shards(acts, incoming, routes, route_weight, norm_gain, w_gate, w_up, w_down):
        ticks, _, tokens, _ = routes.shape
        width, hidden = w_gate.shape[1:]
        chunks = CHUNKS
        cols = width // chunks
        lanes = -(-tokens // 128) * 128
        table = -(-ticks * EXPERTS // 8) * 8
        half = jnp.bfloat16
        anywhere = pl.BlockSpec(memory_space=pl.ANY)
        vmem = pl.BlockSpec(memory_space=pltpu.VMEM)
        dma = pltpu.SemaphoreType.DMA
        result = pl.pallas_call(
            functools.partial(kernel, n, sections),
            out_shape=jax.ShapeDtypeStruct((ticks, tokens, width), half),
            in_specs=[anywhere, anywhere, vmem, vmem, vmem, anywhere, anywhere, anywhere],
            out_specs=vmem,
            scratch_shapes=[
                pltpu.VMEM((width, hidden), half),
                pltpu.VMEM((width, hidden), half),
                pltpu.VMEM((hidden, width), half),
                pltpu.VMEM((ticks, n, chunks, tokens, cols), half),
                pltpu.VMEM((n, table, lanes), jnp.float32),
                pltpu.VMEM((2, ticks, n, chunks, tokens, cols), half),
                pltpu.VMEM((ticks, n, chunks, tokens, cols), half),
                pltpu.VMEM((n, chunks, tokens, cols), jnp.float32),
                pltpu.VMEM((ticks - 1, chunks, tokens, cols), half),
                dma((3, PIECES)),
                dma((chunks,)),
                dma((ticks, chunks)),
                dma((2, ticks, n, chunks)),
                dma((2, ticks, n, chunks)),
                dma((2, n)),
                dma((2, n)),
                dma((2, ticks, n, chunks)),
                dma((2, ticks, n, chunks)),
                dma((ticks - 1, chunks)),
                dma((ticks - 1, chunks)),
            ],
            compiler_params=pltpu.CompilerParams(
                collective_id=0, has_side_effects=True, vmem_limit_bytes=56 << 20
            ),
        )(
            acts[0],
            incoming,
            jnp.swapaxes(routes, 2, 3),
            jnp.swapaxes(route_weight, 2, 3),
            norm_gain,
            w_gate[0],
            w_up[0],
            w_down[0],
        )
        return result[:, None]

    return jax.shard_map(
        shards,
        mesh=mesh,
        in_specs=(
            P("section", "expert", None),
            P(None, "expert", None),
            P(None, "section", "expert", None),
            P(None, "section", "expert", None),
            P("section", None),
            P("section", None, "expert"),
            P("section", None, "expert"),
            P("section", "expert", None),
        ),
        out_specs=P(None, "section", "expert", None),
        check_vma=False,
    )
```

profile of v0, /device:TPU:0, one launch (start us, length us, event | category | flops | bytes accessed | tf_op | source)
XLA Modules:
  0.0 64.7 jit_solution(13759441306266922830)
XLA Ops:
  0.0 63.0 %shard_map.82 = bf16[2,32,2560]{2,1,0:T(8,128)(2,1)} custom-call(bf16[32,2560]{1,0:T(8,128)(2,1)} %bitcast.13, bf16[1,32,2560]{2,1,0:T(8,128)(2,1)} %incoming.1, s32[2,1,2,32]{3,2,1,0:T(2,128)} %bitcast.14, f32[2,1,2,32]{3,2,1,0:T(2,128)} %bitcast.15, f32[1,2560]{1,0:T(1,128)} %gain.1, bf16[2560,768]{1,0:T(8,128)(2,1)} %bitcast.9, ...), custom_call_target="tpu_custom_call" | custom-call | tf_op jit(solution)/shard_map/pallas_call | solution.py:402
  63.0 1.7 %copy.11 = bf16[2,1,32,2560]{3,2,1,0:T(8,128)(2,1)} copy(bf16[2,1,32,2560]{3,2,1,0:T(8,128)(2,1)} %bitcast.12) | data formatting | bytes 655360
where the time goes:
time: 64.9 us; the launch traced here: 64.7 us
  Pallas kernels  63 us (97%)
  local copies, waits for them, and re-layouts  1.72 us (3%)
    pallas_call x1, Pallas kernels, shards(): pl.pallas_call(functools.partial(kernel, n, sections), out_shape=jax.Shap...  63 us
    unnamed x1, local copies, waits for them, and re-layouts  1.72 us

commit v1 on v0

v1 whole, which is shorter than its diff:
```python
import functools

import jax
import jax.numpy as jnp
from jax import lax
from jax.experimental import pallas as pl
from jax.experimental.pallas import tpu as pltpu
from jax.sharding import PartitionSpec as P

MESH = pl.DeviceIdType.MESH
EXPERTS = 4
CAP = 24


def kernel(
    n,
    sections,
    acts,
    incoming,
    routes,
    route_weight,
    gain,
    w_gate_hbm,
    w_up_hbm,
    w_down_hbm,
    out,
    w_gate,
    w_up,
    w_down,
    xown,
    moved,
    xsend,
    xrecv,
    psend,
    precv,
    sel_out,
    sel_in,
    pick,
    w_sem,
    own_sem,
    sel_send,
    sel_recv,
    raw_send,
    raw_recv,
    x_send,
    x_recv,
    p_send,
    p_recv,
):
    s = lax.axis_index("section")
    e = lax.axis_index("expert")
    ticks, chunks, tokens, cols = xown.shape
    top = routes.shape[2]
    cap = xsend.shape[3]
    group = n // EXPERTS
    width = chunks * cols
    rows = n * cap
    has_next = s < sections - 1
    has_prev = s > 0
    following = jnp.minimum(s + 1, sections - 1)
    previous = jnp.maximum(s - 1, 0)
    half = jnp.bfloat16
    single = jnp.float32

    def others(body):
        def step(i, _):
            k = n - 1 - i
            for d, there in ((e + k, e + k < n), (e - k, e - k >= 0)):

                @pl.when(there)
                def _():
                    body(jnp.clip(d, 0, n - 1))

            return 0

        lax.fori_loop(0, n - 1, step, 0)

    def own_copy(t, c):
        source = acts if t == 0 else incoming.at[t - 1]
        return pltpu.make_async_copy(
            source.at[:, pl.ds(c * cols, cols)], xown.at[t, c], own_sem.at[t, c]
        )

    def gate_copy(c):
        span = pl.ds(c * cols, cols)
        return (
            pltpu.make_async_copy(w_gate_hbm.at[span], w_gate.at[span], w_sem.at[0, c]),
            pltpu.make_async_copy(w_up_hbm.at[span], w_up.at[span], w_sem.at[1, c]),
        )

    down_copy = pltpu.make_async_copy(w_down_hbm, w_down, w_sem.at[2, 0])

    def sel_copy(t):
        return pltpu.make_async_remote_copy(
            sel_out.at[t],
            sel_in.at[t],
            sel_send.at[t],
            sel_recv.at[t],
            device_id=(previous, e),
            device_id_type=MESH,
        )

    def raw_copy(t, c):
        return pltpu.make_async_remote_copy(
            moved.at[t, c],
            xown.at[t + 1, c],
            raw_send.at[t, c],
            raw_recv.at[t, c],
            device_id=(following, e),
            device_id_type=MESH,
        )

    def x_copy(slot, t, c, section, d):
        return pltpu.make_async_remote_copy(
            xsend.at[slot, c, d // group],
            xrecv.at[t, c, e],
            x_send.at[slot, c, d],
            x_recv.at[t, c, e],
            device_id=(section, d),
            device_id_type=MESH,
        )

    def x_arrival(t, c, d):
        return pltpu.make_async_remote_copy(
            xrecv.at[t, c, d],
            xrecv.at[t, c, d],
            x_send.at[0, c, d],
            x_recv.at[t, c, d],
            device_id=(s, d),
            device_id_type=MESH,
        )

    def p_copy(t, c, d):
        return pltpu.make_async_remote_copy(
            psend.at[t, c, d],
            precv.at[t, c, e],
            p_send.at[t, c, d],
            p_recv.at[t, c, e],
            device_id=(s, d),
            device_id_type=MESH,
        )

    def p_arrival(t, c, d):
        return pltpu.make_async_remote_copy(
            precv.at[t, c, d],
            precv.at[t, c, d],
            p_send.at[t, c, d],
            p_recv.at[t, c, d],
            device_id=(s, d),
            device_id_type=MESH,
        )

    for c in range(chunks):
        own_copy(0, c).start()

    barrier = pltpu.get_barrier_semaphore()

    def greet(d, _):
        @pl.when(d != e)
        def _():
            pl.semaphore_signal(barrier, inc=1, device_id=(s, d), device_id_type=MESH)

        @pl.when(has_next)
        def _():
            pl.semaphore_signal(barrier, inc=1, device_id=(following, d), device_id_type=MESH)

        @pl.when(has_prev)
        def _():
            pl.semaphore_signal(barrier, inc=1, device_id=(previous, d), device_id_type=MESH)

        return 0

    lax.fori_loop(0, n, greet, 0)

    for c in range(chunks):
        for copy in gate_copy(c):
            copy.start()
    down_copy.start()

    @pl.when(jnp.logical_not(has_prev))
    def _():
        for t in range(1, ticks):
            for c in range(chunks):
                own_copy(t, c).start()

    def iota(shape, axis):
        return lax.broadcasted_iota(jnp.int32, shape, axis)

    before = (iota((tokens, tokens), 0) < iota((tokens, tokens), 1)).astype(half)
    diagonal = iota((tokens, tokens), 0) == iota((tokens, tokens), 1)
    sel_first = None
    for t in range(ticks):
        chosen = routes[t, 0]
        hot = sum(
            (iota((EXPERTS, tokens), 0) == chosen[k : k + 1]).astype(single) for k in range(top)
        )
        rank = jnp.dot(hot.astype(half), before, preferred_element_type=single)
        place = iota((cap, tokens), 0).astype(single)
        whole = None
        for k in range(top):
            blocks = []
            for x in range(EXPERTS):
                slot = jnp.where(chosen[k : k + 1] == x, rank[x : x + 1], -1.0)
                blocks.append((place == slot).astype(single))
            spread = jnp.concatenate([b for b in blocks for _ in range(group)], axis=0)
            pick[t, k * tokens : (k + 1) * tokens, :] = lax.dot_general(
                diagonal.astype(half),
                spread.astype(half),
                (((1,), (1,)), ((), ())),
                preferred_element_type=single,
            ).astype(half)
            mine = jnp.concatenate(blocks, axis=0)
            whole = mine if whole is None else whole + mine
        if t == 0:
            sel_first = whole.astype(half)
        else:
            sel_out[t - 1] = whole.astype(half)

    pl.semaphore_wait(
        barrier, n - 1 + jnp.where(has_next, n, 0) + jnp.where(has_prev, n, 0)
    )

    def pack(slot, c, sel, value):
        packed = jnp.dot(sel, value, preferred_element_type=single)
        for x in range(EXPERTS):
            xsend[slot, c, x] = packed[x * cap : (x + 1) * cap].astype(half)

    def keep(slot, t, c):
        xrecv[t, c, e] = xsend[slot, c, e // group]

    for c in range(chunks):
        own_copy(0, c).wait()
        pack(0, c, sel_first, xown[0, c])
        others(lambda d: x_copy(0, 0, c, s, d).start())
        keep(0, 0, c)

    @pl.when(has_prev)
    def _():
        for t in range(ticks - 1):
            sel_copy(t).start()

    def stack(ref, t, c):
        return jnp.concatenate([ref[t, c, d].astype(single) for d in range(n)], axis=0)

    for t in range(ticks):
        gate_val = up_val = None
        squares = jnp.zeros((rows, 1), single)
        for c in range(chunks):
            if t == 0:
                others(lambda d: x_arrival(t, c, d).wait_recv())
                for copy in gate_copy(c):
                    copy.wait()
            else:

                def arrive(d, _):
                    @pl.when(jnp.logical_or(has_prev, d != e))
                    def _():
                        x_arrival(t, c, d).wait_recv()

                    return 0

                lax.fori_loop(0, n, arrive, 0)
            span = pl.ds(c * cols, cols)
            value = stack(xrecv, t, c)
            squares = squares + jnp.sum(value * value, axis=1, keepdims=True)
            normed = (value * gain[:, span]).astype(half)
            gate_part = jnp.dot(normed, w_gate[span, :], preferred_element_type=single)
            up_part = jnp.dot(normed, w_up[span, :], preferred_element_type=single)
            gate_val = gate_part if gate_val is None else gate_val + gate_part
            up_val = up_part if up_val is None else up_val + up_part
        scale = lax.rsqrt(squares * (1.0 / width) + 1e-06)
        hidden = (jax.nn.silu(gate_val * scale) * (up_val * scale)).astype(half)
        if t == 0:
            down_copy.wait()
        for c in range(chunks):
            span = pl.ds(c * cols, cols)
            value = jnp.dot(hidden, w_down[:, span], preferred_element_type=single)
            for d in range(n):
                psend[t, c, d] = value[d * cap : (d + 1) * cap].astype(half)
            others(lambda d: p_copy(t, c, d).start())
            precv[t, c, e] = psend[t, c, e]

        if t < ticks - 1:

            @pl.when(jnp.logical_not(has_prev))
            def _():
                for c in range(chunks):
                    own_copy(t + 1, c).wait()
                    pack(t + 1, c, sel_out[t], xown[t + 1, c])
                    others(lambda d: x_copy(t + 1, t + 1, c, s, d).start())
                    keep(t + 1, t + 1, c)

            @pl.when(has_next)
            def _():
                sel_copy(t).wait_recv()

        weights = [
            jnp.sum(
                jnp.where(diagonal, route_weight[t, 0][k : k + 1], 0.0), axis=1, keepdims=True
            )
            for k in range(top)
        ]
        for c in range(chunks):
            if t > 0:

                @pl.when(has_prev)
                def _():
                    raw_copy(t - 1, c).wait_recv()

            others(lambda d: p_arrival(t, c, d).wait_recv())
            back = jnp.dot(
                pick[t], stack(precv, t, c).astype(half), preferred_element_type=single
            )
            layer = xown[t, c].astype(single)
            for k in range(top):
                layer = layer + back[k * tokens : (k + 1) * tokens] * weights[k]
            layer = layer.astype(half)
            out[t, :, pl.ds(c * cols, cols)] = layer
            if t < ticks - 1:

                @pl.when(has_next)
                def _():
                    pack(ticks + t, c, sel_in[t], layer)

                    def forward(i, _):
                        x_copy(ticks + t, t + 1, c, following, i).start()
                        return 0

                    lax.fori_loop(0, n, forward, 0)
                    moved[t, c] = layer
                    raw_copy(t, c).start()

    def drain(d, _):
        for c in range(chunks):

            @pl.when(d != e)
            def _():
                x_copy(0, 0, c, s, d).wait_send()
                for t in range(ticks):
                    p_copy(t, c, d).wait_send()

            @pl.when(jnp.logical_and(d != e, jnp.logical_not(has_prev)))
            def _():
                for t in range(1, ticks):
                    x_copy(t, t, c, s, d).wait_send()

            @pl.when(has_next)
            def _():
                for t in range(ticks - 1):
                    x_copy(ticks + t, t + 1, c, following, d).wait_send()

        return 0

    lax.fori_loop(0, n, drain, 0)

    for t in range(ticks - 1):

        @pl.when(has_next)
        def _():
            for c in range(chunks):
                raw_copy(t, c).wait_send()

        @pl.when(has_prev)
        def _():
            sel_copy(t).wait_send()


def solution(mesh):
    n = mesh.shape["expert"]
    sections = mesh.shape["section"]

    def shards(acts, incoming, routes, route_weight, norm_gain, w_gate, w_up, w_down):
        ticks, _, tokens, _ = routes.shape
        width, hidden = w_gate.shape[1:]
        chunks = 5 if width % (5 * 128) == 0 else 4
        cols = width // chunks
        cap = min(CAP, tokens)
        half = jnp.bfloat16
        anywhere = pl.BlockSpec(memory_space=pl.ANY)
        vmem = pl.BlockSpec(memory_space=pltpu.VMEM)
        dma = pltpu.SemaphoreType.DMA
        moves = max(ticks - 1, 1)
        result = pl.pallas_call(
            functools.partial(kernel, n, sections),
            out_shape=jax.ShapeDtypeStruct((ticks, tokens, width), half),
            in_specs=[anywhere, anywhere, vmem, vmem, vmem, anywhere, anywhere, anywhere],
            out_specs=vmem,
            scratch_shapes=[
                pltpu.VMEM((width, hidden), half),
                pltpu.VMEM((width, hidden), half),
                pltpu.VMEM((hidden, width), half),
                pltpu.VMEM((ticks, chunks, tokens, cols), half),
                pltpu.VMEM((moves, chunks, tokens, cols), half),
                pltpu.VMEM((2 * ticks - 1, chunks, EXPERTS, cap, cols), half),
                pltpu.VMEM((ticks, chunks, n, cap, cols), half),
                pltpu.VMEM((ticks, chunks, n, cap, cols), half),
                pltpu.VMEM((ticks, chunks, n, cap, cols), half),
                pltpu.VMEM((moves, EXPERTS * cap, tokens), half),
                pltpu.VMEM((moves, EXPERTS * cap, tokens), half),
                pltpu.VMEM((ticks, routes.shape[3] * tokens, n * cap), half),
                dma((3, chunks)),
                dma((ticks, chunks)),
                dma((moves,)),
                dma((moves,)),
                dma((moves, chunks)),
                dma((moves, chunks)),
                dma((2 * ticks - 1, chunks, n)),
                dma((ticks, chunks, n)),
                dma((ticks, chunks, n)),
                dma((ticks, chunks, n)),
            ],
            compiler_params=pltpu.CompilerParams(
                collective_id=0, has_side_effects=True, vmem_limit_bytes=56 << 20
            ),
        )(
            acts[0],
            incoming,
            jnp.swapaxes(routes, 2, 3),
            jnp.swapaxes(route_weight, 2, 3),
            norm_gain,
            w_gate[0],
            w_up[0],
            w_down[0],
        )
        return result[:, None]

    return jax.shard_map(
        shards,
        mesh=mesh,
        in_specs=(
            P("section", "expert", None),
            P(None, "expert", None),
            P(None, "section", "expert", None),
            P(None, "section", "expert", None),
            P("section", None),
            P("section", None, "expert"),
            P("section", None, "expert"),
            P("section", "expert", None),
        ),
        out_specs=P(None, "section", "expert", None),
        check_vma=False,
    )
```

time: 64.9 us -> 62.3 us (0.960)
  Pallas kernels: 63 us -> 59.9 us
    pallas_call x1, Pallas kernels: 63 us -> 59.9 us  [shards(): pl.pallas_call(functools.partial(kernel, n, sections), out_shape=jax.Shap...]
where the time goes in v1:
time: 62.3 us; the launch traced here: 61.7 us
  Pallas kernels  59.9 us (96%)
  local copies, waits for them, and re-layouts  1.72 us (3%)
    pallas_call x1, Pallas kernels, shards(): pl.pallas_call(functools.partial(kernel, n, sections), out_shape=jax.Shap...  59.9 us
    unnamed x1, local copies, waits for them, and re-layouts  1.72 us

profile of v1, /device:TPU:0, one launch (start us, length us, event | category | flops | bytes accessed | tf_op | source)
XLA Modules:
  0.0 61.7 jit_solution(12738940903021476108)
XLA Ops:
  0.0 59.9 %shard_map.82 = bf16[2,32,2560]{2,1,0:T(8,128)(2,1)} custom-call(bf16[32,2560]{1,0:T(8,128)(2,1)} %bitcast.13, bf16[1,32,2560]{2,1,0:T(8,128)(2,1)} %incoming.1, s32[2,1,2,32]{3,2,1,0:T(2,128)} %bitcast.14, f32[2,1,2,32]{3,2,1,0:T(2,128)} %bitcast.15, f32[1,2560]{1,0:T(1,128)} %gain.1, bf16[2560,768]{1,0:T(8,128)(2,1)} %bitcast.9, ...), custom_call_target="tpu_custom_call" | custom-call | tf_op jit(solution)/shard_map/pallas_call | solution.py:383
  59.9 1.7 %copy.11 = bf16[2,1,32,2560]{3,2,1,0:T(8,128)(2,1)} copy(bf16[2,1,32,2560]{3,2,1,0:T(8,128)(2,1)} %bitcast.12) | data formatting | bytes 655360

commit v2 on v1

--- a/solution.py
+++ b/solution.py
@@ -46,6 +46,7 @@
     x_recv,
     p_send,
     p_recv,
+    turn,
 ):
     s = lax.axis_index("section")
     e = lax.axis_index("expert")
@@ -228,6 +229,14 @@
     def keep(slot, t, c):
         xrecv[t, c, e] = xsend[slot, c, e // group]
 
+    paired = sections % 2 == 0
+    leads = lax.rem(s, 2) == 0
+    if paired:
+
+        @pl.when(jnp.logical_not(leads))
+        def _():
+            pl.semaphore_wait(turn, 1)
+
     for c in range(chunks):
         own_copy(0, c).wait()
         pack(0, c, sel_first, xown[0, c])
@@ -238,6 +247,14 @@
     def _():
         for t in range(ticks - 1):
             sel_copy(t).start()
+
+    for c in range(chunks):
+        others(lambda d: x_copy(0, 0, c, s, d).wait_send())
+    if paired:
+
+        @pl.when(leads)
+        def _():
+            pl.semaphore_signal(turn, inc=1, device_id=(following, e), device_id_type=MESH)
 
     def stack(ref, t, c):
         return jnp.concatenate([ref[t, c, d].astype(single) for d in range(n)], axis=0)
@@ -335,7 +352,6 @@
 
             @pl.when(d != e)
             def _():
-                x_copy(0, 0, c, s, d).wait_send()
                 for t in range(ticks):
                     p_copy(t, c, d).wait_send()
 
@@ -408,6 +424,7 @@
                 dma((ticks, chunks, n)),
                 dma((ticks, chunks, n)),
                 dma((ticks, chunks, n)),
+                pltpu.SemaphoreType.REGULAR,
             ],
             compiler_params=pltpu.CompilerParams(
                 collective_id=0, has_side_effects=True, vmem_limit_bytes=56 << 20

time: 62.3 us -> 60 us (0.963)
  the two profiles are of different devices: /device:TPU:0 before, /device:TPU:1 now
where the time goes in v2:
time: 60 us; the launch traced here: 59.7 us
  Pallas kernels  58 us (97%)
  local copies, waits for them, and re-layouts  1.72 us (3%)
    pallas_call x1, Pallas kernels, shards(): pl.pallas_call(functools.partial(kernel, n, sections), out_shape=jax.Shap...  58 us
    unnamed x1, local copies, waits for them, and re-layouts  1.72 us

profile of v2, /device:TPU:1, one launch (start us, length us, event | category | flops | bytes accessed | tf_op | source)
XLA Modules:
  0.0 59.7 jit_solution(13681459689219782092)
XLA Ops:
  0.0 58.0 %shard_map.82 = bf16[2,32,2560]{2,1,0:T(8,128)(2,1)} custom-call(bf16[32,2560]{1,0:T(8,128)(2,1)} %bitcast.13, bf16[1,32,2560]{2,1,0:T(8,128)(2,1)} %incoming.1, s32[2,1,2,32]{3,2,1,0:T(2,128)} %bitcast.14, f32[2,1,2,32]{3,2,1,0:T(2,128)} %bitcast.15, f32[1,2560]{1,0:T(1,128)} %gain.1, bf16[2560,768]{1,0:T(8,128)(2,1)} %bitcast.9, ...), custom_call_target="tpu_custom_call" | custom-call | tf_op jit(solution)/shard_map/pallas_call | solution.py:399
  58.0 1.7 %copy.11 = bf16[2,1,32,2560]{3,2,1,0:T(8,128)(2,1)} copy(bf16[2,1,32,2560]{3,2,1,0:T(8,128)(2,1)} %bitcast.12) | data formatting | bytes 655360

commit v3 on v2

--- a/solution.py
+++ b/solution.py
@@ -161,17 +161,14 @@
         def _():
             pl.semaphore_signal(barrier, inc=1, device_id=(s, d), device_id_type=MESH)
 
-        @pl.when(has_next)
-        def _():
-            pl.semaphore_signal(barrier, inc=1, device_id=(following, d), device_id_type=MESH)
-
-        @pl.when(has_prev)
-        def _():
-            pl.semaphore_signal(barrier, inc=1, device_id=(previous, d), device_id_type=MESH)
-
         return 0
 
     lax.fori_loop(0, n, greet, 0)
+    for there, section in ((has_next, following), (has_prev, previous)):
+
+        @pl.when(there)
+        def _():
+            pl.semaphore_signal(barrier, inc=1, device_id=(section, e), device_id_type=MESH)
 
     for c in range(chunks):
         for copy in gate_copy(c):
@@ -218,7 +215,7 @@
             sel_out[t - 1] = whole.astype(half)
 
     pl.semaphore_wait(
-        barrier, n - 1 + jnp.where(has_next, n, 0) + jnp.where(has_prev, n, 0)
+        barrier, n - 1 + jnp.where(has_next, 1, 0) + jnp.where(has_prev, 1, 0)
     )
 
     def pack(slot, c, sel, value):
@@ -299,14 +296,6 @@
 
         if t < ticks - 1:
 
-            @pl.when(jnp.logical_not(has_prev))
-            def _():
-                for c in range(chunks):
-                    own_copy(t + 1, c).wait()
-                    pack(t + 1, c, sel_out[t], xown[t + 1, c])
-                    others(lambda d: x_copy(t + 1, t + 1, c, s, d).start())
-                    keep(t + 1, t + 1, c)
-
             @pl.when(has_next)
             def _():
                 sel_copy(t).wait_recv()
@@ -346,6 +335,16 @@
                     lax.fori_loop(0, n, forward, 0)
                     moved[t, c] = layer
                     raw_copy(t, c).start()
+
+        if t < ticks - 1:
+
+            @pl.when(jnp.logical_not(has_prev))
+            def _():
+                for c in range(chunks):
+                    own_copy(t + 1, c).wait()
+                    pack(t + 1, c, sel_out[t], xown[t + 1, c])
+                    others(lambda d: x_copy(t + 1, t + 1, c, s, d).start())
+                    keep(t + 1, t + 1, c)
 
     def drain(d, _):
         for c in range(chunks):

time: 60 us -> 61.2 us (1.020)
  the two profiles are of different devices: /device:TPU:1 before, /device:TPU:0 now
where the time goes in v3:
time: 61.2 us; the launch traced here: 60.9 us
  Pallas kernels  59.2 us (97%)
  local copies, waits for them, and re-layouts  1.72 us (3%)
    pallas_call x1, Pallas kernels, shards(): pl.pallas_call(functools.partial(kernel, n, sections), out_shape=jax.Shap...  59.2 us
    unnamed x1, local copies, waits for them, and re-layouts  1.72 us

profile of v3, /device:TPU:0, one launch (start us, length us, event | category | flops | bytes accessed | tf_op | source)
XLA Modules:
  0.0 60.9 jit_solution(10989947695111302592)
XLA Ops:
  0.0 59.2 %shard_map.82 = bf16[2,32,2560]{2,1,0:T(8,128)(2,1)} custom-call(bf16[32,2560]{1,0:T(8,128)(2,1)} %bitcast.13, bf16[1,32,2560]{2,1,0:T(8,128)(2,1)} %incoming.1, s32[2,1,2,32]{3,2,1,0:T(2,128)} %bitcast.14, f32[2,1,2,32]{3,2,1,0:T(2,128)} %bitcast.15, f32[1,2560]{1,0:T(1,128)} %gain.1, bf16[2560,768]{1,0:T(8,128)(2,1)} %bitcast.9, ...), custom_call_target="tpu_custom_call" | custom-call | tf_op jit(solution)/shard_map/pallas_call | solution.py:398
  59.2 1.7 %copy.11 = bf16[2,1,32,2560]{3,2,1,0:T(8,128)(2,1)} copy(bf16[2,1,32,2560]{3,2,1,0:T(8,128)(2,1)} %bitcast.12) | data formatting | bytes 655360

commit v4 on v3

v4 whole, which is shorter than its diff:
```python
import functools

import jax
import jax.numpy as jnp
from jax import lax
from jax.experimental import pallas as pl
from jax.experimental.pallas import tpu as pltpu
from jax.sharding import PartitionSpec as P

MESH = pl.DeviceIdType.MESH
EXPERTS = 4
CAP = 24


def kernel(
    n,
    sections,
    acts,
    incoming,
    routes,
    route_weight,
    gain,
    w_gate_hbm,
    w_up_hbm,
    w_down_hbm,
    out,
    w_gate,
    w_up,
    w_down,
    xown,
    moved,
    xsend,
    xraw,
    xrelay,
    xrecv,
    psend,
    precv,
    pgate,
    fsend,
    frecv,
    sel,
    sel_in,
    sel_far,
    pick,
    pick_far,
    rate,
    rate_far,
    w_sem,
    own_sem,
    table_send,
    table_recv,
    sel_send,
    sel_recv,
    raw_send,
    raw_recv,
    far_send,
    far_recv,
    x_send,
    x_recv,
    relay_send,
    p_send,
    p_recv,
    gate_send,
    gate_recv,
    f_send,
    f_recv,
    turn,
):
    s = lax.axis_index("section")
    e = lax.axis_index("expert")
    ticks, chunks, tokens, cols = xown.shape
    top = routes.shape[2]
    cap = xrecv.shape[3]
    group = n // EXPERTS
    mid = n // 2
    sided = EXPERTS // 2
    width = chunks * cols
    rows = n * cap
    side = e // mid
    base, far_base = side * mid, (1 - side) * mid
    own = e - base
    near_gate = jnp.where(side == 0, mid - 1, mid)
    far_gate = jnp.where(side == 0, mid, mid - 1)
    is_gate = e == near_gate
    not_gate = e != near_gate
    has_next = s < sections - 1
    has_prev = s > 0
    following = jnp.minimum(s + 1, sections - 1)
    previous = jnp.maximum(s - 1, 0)
    half = jnp.bfloat16
    single = jnp.float32

    def remote(source, target, send, recv, section, device):
        return pltpu.make_async_remote_copy(
            source, target, send, recv, device_id=(section, device), device_id_type=MESH
        )

    def near(body, own_too=False):
        def step(i, _):
            body(base + lax.rem(own + i, mid))
            return 0

        lax.fori_loop(0 if own_too else 1, mid, step, 0)

    def own_copy(t, c):
        source = acts if t == 0 else incoming.at[t - 1]
        return pltpu.make_async_copy(
            source.at[:, pl.ds(c * cols, cols)], xown.at[t, c], own_sem.at[t, c]
        )

    def gate_copy(c):
        span = pl.ds(c * cols, cols)
        return (
            pltpu.make_async_copy(w_gate_hbm.at[span], w_gate.at[span], w_sem.at[0, c]),
            pltpu.make_async_copy(w_up_hbm.at[span], w_up.at[span], w_sem.at[1, c]),
        )

    down_copy = pltpu.make_async_copy(w_down_hbm, w_down, w_sem.at[2, 0])

    def table_copies(t):
        pairs = (
            (sel.at[t, 1 - side], sel_far),
            (pick.at[t, 1 - side], pick_far),
            (rate.at[t], rate_far),
        )
        return [
            remote(
                source,
                target.at[t, own],
                table_send.at[i, t],
                table_recv.at[i, t, own],
                s,
                far_gate,
            )
            for i, (source, target) in enumerate(pairs)
        ]

    def table_arrival(i, t, j):
        target = (sel_far, pick_far, rate_far)[i].at[t, j]
        return remote(target, target, table_send.at[i, t], table_recv.at[i, t, j], s, far_base + j)

    def sel_copy(t):
        return remote(
            sel.at[t + 1, side], sel_in.at[t], sel_send.at[t], sel_recv.at[t], previous, e
        )

    def raw_copy(t, c):
        return remote(
            moved.at[t, c], xown.at[t + 1, c], raw_send.at[t, c], raw_recv.at[t, c], following, e
        )

    def far_copy(slot, t, c, section, source):
        return remote(
            source, xraw.at[t, c, own], far_send.at[slot, c], far_recv.at[t, c, own], section, far_gate
        )

    def far_arrival(t, c, j):
        target = xraw.at[t, c, j]
        return remote(target, target, far_send.at[0, c], far_recv.at[t, c, j], s, far_base + j)

    def x_copy(slot, t, c, section, d):
        return remote(
            xsend.at[slot, c, d // group - side * sided],
            xrecv.at[t, c, e],
            x_send.at[slot, c, d - base],
            x_recv.at[t, c, e],
            section,
            d,
        )

    def relay_copy(t, c, j, d):
        return remote(
            xrelay.at[t, c, j, d // group - side * sided],
            xrecv.at[t, c, far_base + j],
            relay_send.at[t, c, j, d - base],
            x_recv.at[t, c, far_base + j],
            s,
            d,
        )

    def x_arrival(t, c, d):
        target = xrecv.at[t, c, d]
        return remote(target, target, x_send.at[0, c, 0], x_recv.at[t, c, d], s, d)

    def p_copy(t, c, d):
        return remote(
            psend.at[t, c, side, d - base],
            precv.at[t, c, own],
            p_send.at[t, c, d - base],
            p_recv.at[t, c, own],
            s,
            d,
        )

    def p_arrival(t, c, d):
        target = precv.at[t, c, d - base]
        return remote(target, target, p_send.at[t, c, 0], p_recv.at[t, c, d - base], s, d)

    def gate_send_copy(t, c):
        return remote(
            psend.at[t, c, 1 - side],
            pgate.at[t, c, own],
            gate_send.at[t, c],
            gate_recv.at[t, c, own],
            s,
            near_gate,
        )

    def gate_arrival(t, c, d):
        target = pgate.at[t, c, d - base]
        return remote(target, target, gate_send.at[t, c], gate_recv.at[t, c, d - base], s, d)

    def f_copy(t, c, j):
        return remote(
            fsend.at[t, c, j], frecv.at[t, c], f_send.at[t, c, j], f_recv.at[t, c], s, far_base + j
        )

    for c in range(chunks):
        own_copy(0, c).start()

    barrier = pltpu.get_barrier_semaphore()

    def greet(d, _):
        @pl.when(d != e)
        def _():
            pl.semaphore_signal(barrier, inc=1, device_id=(s, d), device_id_type=MESH)

        return 0

    lax.fori_loop(0, n, greet, 0)
    for there, section in ((has_next, following), (has_prev, previous)):

        @pl.when(there)
        def _():
            pl.semaphore_signal(barrier, inc=1, device_id=(section, e), device_id_type=MESH)

    for c in range(chunks):
        for copy in gate_copy(c):
            copy.start()
    down_copy.start()

    @pl.when(jnp.logical_not(has_prev))
    def _():
        for t in range(1, ticks):
            for c in range(chunks):
                own_copy(t, c).start()

    def iota(shape, axis):
        return lax.broadcasted_iota(jnp.int32, shape, axis)

    before = (iota((tokens, tokens), 0) < iota((tokens, tokens), 1)).astype(half)
    diagonal = iota((tokens, tokens), 0) == iota((tokens, tokens), 1)
    place = iota((cap, tokens), 0).astype(single)
    for t in range(ticks):
        chosen = routes[t, 0]
        hot = sum(
            (iota((EXPERTS, tokens), 0) == chosen[k : k + 1]).astype(single) for k in range(top)
        )
        rank = jnp.dot(hot.astype(half), before, preferred_element_type=single)
        blocks = [
            [
                (place == jnp.where(chosen[k : k + 1] == x, rank[x : x + 1], -1.0)).astype(single)
                for x in range(EXPERTS)
            ]
            for k in range(top)
        ]
        for h in range(2):
            experts = range(h * sided, (h + 1) * sided)
            sel[t, h] = sum(
                jnp.concatenate([blocks[k][x] for x in experts], axis=0) for k in range(top)
            ).astype(half)
            for k in range(top):
                spread = jnp.concatenate(
                    [blocks[k][x] for x in experts for _ in range(group)], axis=0
                )
                pick[t, h, k * tokens : (k + 1) * tokens, :] = lax.dot_general(
                    diagonal.astype(half),
                    spread.astype(half),
                    (((1,), (1,)), ((), ())),
                    preferred_element_type=single,
                ).astype(half)
        rate[t] = jnp.zeros_like(rate[t])
        rate[t, 0:top, 0:tokens] = route_weight[t, 0]

    pl.semaphore_wait(
        barrier, n - 1 + jnp.where(has_next, 1, 0) + jnp.where(has_prev, 1, 0)
    )

    def pack(target, table, value):
        packed = jnp.dot(table, value, preferred_element_type=single)
        for x in range(sided):
            target[x] = packed[x * cap : (x + 1) * cap].astype(half)

    def dispatch(t, c):
        own_copy(t, c).wait()
        far_copy(t, t, c, s, xown.at[t, c]).start()
        pack(xsend.at[t, c], sel[t, side], xown[t, c])
        near(lambda d: x_copy(t, t, c, s, d).start())
        xrecv[t, c, e] = xsend[t, c, e // group - side * sided]

    paired = sections % 2 == 0
    leads = lax.rem(s, 2) == 0
    table_copies(0)[0].start()
    if paired:

        @pl.when(jnp.logical_not(leads))
        def _():
            pl.semaphore_wait(turn, 1)

    for c in range(chunks):
        dispatch(0, c)
    for t in range(ticks):
        for copy in table_copies(t)[1 if t == 0 else 0 :]:
            copy.start()

    @pl.when(has_prev)
    def _():
        for t in range(ticks - 1):
            sel_copy(t).start()

    def pass_turn():
        for c in range(chunks):
            far_copy(0, 0, c, s, xown.at[0, c]).wait_send()
            near(lambda d: x_copy(0, 0, c, s, d).wait_send())
        if paired:

            @pl.when(leads)
            def _():
                pl.semaphore_signal(turn, inc=1, device_id=(following, e), device_id_type=MESH)

    def relay(t, c):
        for j in range(mid):
            if c == 0:
                table_arrival(0, t, j).wait_recv()
            far_arrival(t, c, j).wait_recv()
            pack(xrelay.at[t, c, j], sel_far[t, j], xraw[t, c, j])
            near(lambda d: relay_copy(t, c, j, d).start())
            xrecv[t, c, far_base + j] = xrelay[t, c, j, e // group - side * sided]

    def combine(t, c):
        near(lambda d: gate_arrival(t, c, d).wait_recv())
        for j in range(mid):
            if c == 0:
                table_arrival(1, t, j).wait_recv()
                table_arrival(2, t, j).wait_recv()
            value = jnp.concatenate(
                [pgate[t, c, d, j].astype(single) for d in range(mid)], axis=0
            ).astype(half)
            back = jnp.dot(pick_far[t, j], value, preferred_element_type=single)
            total = None
            for k in range(top):
                part = back[k * tokens : (k + 1) * tokens] * column(rate_far[t, j], k)
                total = part if total is None else total + part
            fsend[t, c, j] = total.astype(half)
            f_copy(t, c, j).start()

    def column(table, k):
        return jnp.sum(
            jnp.where(diagonal, table[k : k + 1, 0:tokens], 0.0), axis=1, keepdims=True
        )

    for t in range(ticks):
        gate_val = up_val = None
        squares = jnp.zeros((rows, 1), single)
        if t == 0:

            @pl.when(not_gate)
            def _():
                pass_turn()

        for c in range(chunks):

            @pl.when(is_gate)
            def _():
                relay(t, c)

            @pl.when(not_gate)
            def _():
                for j in range(mid):
                    x_arrival(t, c, far_base + j).wait_recv()

            near(lambda d: x_arrival(t, c, d).wait_recv())
            if t == 0:
                for copy in gate_copy(c):
                    copy.wait()
            else:

                @pl.when(has_prev)
                def _():
                    x_arrival(t, c, e).wait_recv()

            span = pl.ds(c * cols, cols)
            value = jnp.concatenate([xrecv[t, c, d].astype(single) for d in range(n)], axis=0)
            squares = squares + jnp.sum(value * value, axis=1, keepdims=True)
            normed = (value * gain[:, span]).astype(half)
            gate_part = jnp.dot(normed, w_gate[span, :], preferred_element_type=single)
            up_part = jnp.dot(normed, w_up[span, :], preferred_element_type=single)
            gate_val = gate_part if gate_val is None else gate_val + gate_part
            up_val = up_part if up_val is None else up_val + up_part
        scale = lax.rsqrt(squares * (1.0 / width) + 1e-06)
        hidden = (jax.nn.silu(gate_val * scale) * (up_val * scale)).astype(half)
        if t == 0:

            @pl.when(is_gate)
            def _():
                pass_turn()

            down_copy.wait()
        for c in range(chunks):
            span = pl.ds(c * cols, cols)
            value = jnp.dot(hidden, w_down[:, span], preferred_element_type=single)
            for d in range(n):
                psend[t, c, d // mid, d % mid] = value[d * cap : (d + 1) * cap].astype(half)

            @pl.when(not_gate)
            def _():
                gate_send_copy(t, c).start()

            @pl.when(is_gate)
            def _():
                pgate[t, c, own] = psend[t, c, 1 - side]

            near(lambda d: p_copy(t, c, d).start())
            precv[t, c, own] = psend[t, c, side, own]

        @pl.when(is_gate)
        def _():
            for c in range(chunks):
                combine(t, c)

        if t < ticks - 1:

            @pl.when(has_next)
            def _():
                sel_copy(t).wait_recv()

        weights = [column(rate[t], k) for k in range(top)]
        for c in range(chunks):
            if t > 0:

                @pl.when(has_prev)
                def _():
                    raw_copy(t - 1, c).wait_recv()

            near(lambda d: p_arrival(t, c, d).wait_recv())
            f_copy(t, c, 0).wait_recv()
            value = jnp.concatenate(
                [precv[t, c, d].astype(single) for d in range(mid)], axis=0
            ).astype(half)
            back = jnp.dot(pick[t, side], value, preferred_element_type=single)
            layer = xown[t, c].astype(single) + frecv[t, c].astype(single)
            for k in range(top):
                layer = layer + back[k * tokens : (k + 1) * tokens] * weights[k]
            layer = layer.astype(half)
            out[t, :, pl.ds(c * cols, cols)] = layer
            if t < ticks - 1:

                @pl.when(has_next)
                def _():
                    moved[t, c] = layer
                    far_copy(ticks + t, t + 1, c, following, moved.at[t, c]).start()
                    pack(xsend.at[ticks + t, c], sel_in[t], layer)
                    near(lambda d: x_copy(ticks + t, t + 1, c, following, d).start(), True)
                    raw_copy(t, c).start()

        if t < ticks - 1:
            if paired:

                @pl.when(s == 1)
                def _():
                    pl.semaphore_signal(turn, inc=1, device_id=(previous, e), device_id_type=MESH)

            @pl.when(jnp.logical_not(has_prev))
            def _():
                if paired:
                    pl.semaphore_wait(turn, 1)
                for c in range(chunks):
                    dispatch(t + 1, c)

    for t in range(ticks):
        for copy in table_copies(t):
            copy.wait_send()
        for c in range(chunks):
            near(lambda d: p_copy(t, c, d).wait_send())

            @pl.when(not_gate)
            def _():
                gate_send_copy(t, c).wait_send()

            @pl.when(is_gate)
            def _():
                for j in range(mid):
                    f_copy(t, c, j).wait_send()
                    near(lambda d: relay_copy(t, c, j, d).wait_send())

            if t > 0:

                @pl.when(jnp.logical_not(has_prev))
                def _():
                    far_copy(t, t, c, s, xown.at[t, c]).wait_send()
                    near(lambda d: x_copy(t, t, c, s, d).wait_send())

            if t < ticks - 1:

                @pl.when(has_next)
                def _():
                    far_copy(ticks + t, t + 1, c, following, moved.at[t, c]).wait_send()
                    near(lambda d: x_copy(ticks + t, t + 1, c, following, d).wait_send(), True)
                    raw_copy(t, c).wait_send()

    @pl.when(has_prev)
    def _():
        for t in range(ticks - 1):
            sel_copy(t).wait_send()


def solution(mesh):
    n = mesh.shape["expert"]
    sections = mesh.shape["section"]

    def shards(acts, incoming, routes, route_weight, norm_gain, w_gate, w_up, w_down):
        ticks, _, tokens, top = routes.shape
        width, hidden = w_gate.shape[1:]
        chunks = 5 if width % (5 * 128) == 0 else 4
        cols = width // chunks
        cap = min(CAP, tokens)
        mid, sided, moves = n // 2, EXPERTS // 2, max(ticks - 1, 1)
        half, single = jnp.bfloat16, jnp.float32
        anywhere = pl.BlockSpec(memory_space=pl.ANY)
        vmem = pl.BlockSpec(memory_space=pltpu.VMEM)
        dma = pltpu.SemaphoreType.DMA
        result = pl.pallas_call(
            functools.partial(kernel, n, sections),
            out_shape=jax.ShapeDtypeStruct((ticks, tokens, width), half),
            in_specs=[anywhere, anywhere, vmem, vmem, vmem, anywhere, anywhere, anywhere],
            out_specs=vmem,
            scratch_shapes=[
                pltpu.VMEM((width, hidden), half),
                pltpu.VMEM((width, hidden), half),
                pltpu.VMEM((hidden, width), half),
                pltpu.VMEM((ticks, chunks, tokens, cols), half),
                pltpu.VMEM((moves, chunks, tokens, cols), half),
                pltpu.VMEM((2 * ticks - 1, chunks, sided, cap, cols), half),
                pltpu.VMEM((ticks, chunks, mid, tokens, cols), half),
                pltpu.VMEM((ticks, chunks, mid, sided, cap, cols), half),
                pltpu.VMEM((ticks, chunks, n, cap, cols), half),
                pltpu.VMEM((ticks, chunks, 2, mid, cap, cols), half),
                pltpu.VMEM((ticks, chunks, mid, cap, cols), half),
                pltpu.VMEM((ticks, chunks, mid, mid, cap, cols), half),
                pltpu.VMEM((ticks, chunks, mid, tokens, cols), half),
                pltpu.VMEM((ticks, chunks, tokens, cols), half),
                pltpu.VMEM((ticks, 2, sided * cap, tokens), half),
                pltpu.VMEM((moves, sided * cap, tokens), half),
                pltpu.VMEM((ticks, mid, sided * cap, tokens), half),
                pltpu.VMEM((ticks, 2, top * tokens, mid * cap), half),
                pltpu.VMEM((ticks, mid, top * tokens, mid * cap), half),
                pltpu.VMEM((ticks, 8, 128), single),
                pltpu.VMEM((ticks, mid, 8, 128), single),
                dma((3, chunks)),
                dma((ticks, chunks)),
                dma((3, ticks)),
                dma((3, ticks, mid)),
                dma((moves,)),
                dma((moves,)),
                dma((moves, chunks)),
                dma((moves, chunks)),
                dma((2 * ticks - 1, chunks)),
                dma((ticks, chunks, mid)),
                dma((2 * ticks - 1, chunks, mid)),
                dma((ticks, chunks, n)),
                dma((ticks, chunks, mid, mid)),
                dma((ticks, chunks, mid)),
                dma((ticks, chunks, mid)),
                dma((ticks, chunks)),
                dma((ticks, chunks, mid)),
                dma((ticks, chunks, mid)),
                dma((ticks, chunks)),
                pltpu.SemaphoreType.REGULAR,
            ],
            compiler_params=pltpu.CompilerParams(
                collective_id=0, has_side_effects=True, vmem_limit_bytes=60 << 20
            ),
        )(
            acts[0],
            incoming,
            jnp.swapaxes(routes, 2, 3),
            jnp.swapaxes(route_weight, 2, 3),
            norm_gain,
            w_gate[0],
            w_up[0],
            w_down[0],
        )
        return result[:, None]

    return jax.shard_map(
        shards,
        mesh=mesh,
        in_specs=(
            P("section", "expert", None),
            P(None, "expert", None),
            P(None, "section", "expert", None),
            P(None, "section", "expert", None),
            P("section", None),
            P("section", None, "expert"),
            P("section", None, "expert"),
            P("section", "expert", None),
        ),
        out_specs=P(None, "section", "expert", None),
        check_vma=False,
    )
```

time: 61.2 us -> 59.6 us (0.974)
  Pallas kernels: 59.2 us -> 57.7 us
    pallas_call x1, Pallas kernels: 59.2 us -> 57.7 us  [shards(): pl.pallas_call(functools.partial(kernel, n, sections), out_shape=jax.Shap...]
where the time goes in v4:
time: 59.6 us; the launch traced here: 59.4 us
  Pallas kernels  57.7 us (97%)
  local copies, waits for them, and re-layouts  1.72 us (3%)
    pallas_call x1, Pallas kernels, shards(): pl.pallas_call(functools.partial(kernel, n, sections), out_shape=jax.Shap...  57.7 us
    unnamed x1, local copies, waits for them, and re-layouts  1.72 us

profile of v4, /device:TPU:0, one launch (start us, length us, event | category | flops | bytes accessed | tf_op | source)
XLA Modules:
  0.0 59.4 jit_solution(12725918592341776560)
XLA Ops:
  0.0 57.7 %shard_map.82 = bf16[2,32,2560]{2,1,0:T(8,128)(2,1)} custom-call(bf16[32,2560]{1,0:T(8,128)(2,1)} %bitcast.13, bf16[1,32,2560]{2,1,0:T(8,128)(2,1)} %incoming.1, s32[2,1,2,32]{3,2,1,0:T(2,128)} %bitcast.14, f32[2,1,2,32]{3,2,1,0:T(2,128)} %bitcast.15, f32[1,2560]{1,0:T(1,128)} %gain.1, bf16[2560,768]{1,0:T(8,128)(2,1)} %bitcast.9, ...), custom_call_target="tpu_custom_call" | custom-call | tf_op jit(solution)/shard_map/pallas_call | solution.py:532
  57.7 1.7 %copy.11 = bf16[2,1,32,2560]{3,2,1,0:T(8,128)(2,1)} copy(bf16[2,1,32,2560]{3,2,1,0:T(8,128)(2,1)} %bitcast.12) | data formatting | bytes 655360

commit v5 on v4

--- a/solution.py
+++ b/solution.py
@@ -28,10 +28,8 @@
     w_up,
     w_down,
     xown,
-    moved,
+    made,
     xsend,
-    xraw,
-    xrelay,
     xrecv,
     psend,
     precv,
@@ -40,12 +38,12 @@
     frecv,
     sel,
     sel_in,
-    sel_far,
     pick,
     pick_far,
     rate,
     rate_far,
     w_sem,
+    out_sem,
     own_sem,
     table_send,
     table_recv,
@@ -53,11 +51,8 @@
     sel_recv,
     raw_send,
     raw_recv,
-    far_send,
-    far_recv,
     x_send,
     x_recv,
-    relay_send,
     p_send,
     p_recv,
     gate_send,
@@ -74,6 +69,7 @@
     group = n // EXPERTS
     mid = n // 2
     sided = EXPERTS // 2
+    gated = [t < ticks - 1 for t in range(ticks)]
     width = chunks * cols
     rows = n * cap
     side = e // mid
@@ -102,6 +98,13 @@
 
         lax.fori_loop(0 if own_too else 1, mid, step, 0)
 
+    def far(body):
+        def step(i, _):
+            body(far_base + i)
+            return 0
+
+        lax.fori_loop(0, mid, step, 0)
+
     def own_copy(t, c):
         source = acts if t == 0 else incoming.at[t - 1]
         return pltpu.make_async_copy(
@@ -118,11 +121,7 @@
     down_copy = pltpu.make_async_copy(w_down_hbm, w_down, w_sem.at[2, 0])
 
     def table_copies(t):
-        pairs = (
-            (sel.at[t, 1 - side], sel_far),
-            (pick.at[t, 1 - side], pick_far),
-            (rate.at[t], rate_far),
-        )
+        pairs = ((pick.at[t, 1 - side], pick_far), (rate.at[t], rate_far))
         return [
             remote(
                 source,
@@ -136,69 +135,50 @@
         ]
 
     def table_arrival(i, t, j):
-        target = (sel_far, pick_far, rate_far)[i].at[t, j]
+        target = (pick_far, rate_far)[i].at[t, j]
         return remote(target, target, table_send.at[i, t], table_recv.at[i, t, j], s, far_base + j)
+
+    def out_copy(t, c):
+        return pltpu.make_async_copy(
+            made.at[t, c], out.at[t, :, pl.ds(c * cols, cols)], out_sem.at[t, c]
+        )
 
     def sel_copy(t):
         return remote(
-            sel.at[t + 1, side], sel_in.at[t], sel_send.at[t], sel_recv.at[t], previous, e
+            sel.at[t + 1], sel_in.at[t], sel_send.at[t], sel_recv.at[t], previous, e
         )
 
     def raw_copy(t, c):
         return remote(
-            moved.at[t, c], xown.at[t + 1, c], raw_send.at[t, c], raw_recv.at[t, c], following, e
-        )
-
-    def far_copy(slot, t, c, section, source):
-        return remote(
-            source, xraw.at[t, c, own], far_send.at[slot, c], far_recv.at[t, c, own], section, far_gate
-        )
-
-    def far_arrival(t, c, j):
-        target = xraw.at[t, c, j]
-        return remote(target, target, far_send.at[0, c], far_recv.at[t, c, j], s, far_base + j)
+            made.at[t, c], xown.at[t + 1, c], raw_send.at[t, c], raw_recv.at[t, c], following, e
+        )
 
     def x_copy(slot, t, c, section, d):
         return remote(
-            xsend.at[slot, c, d // group - side * sided],
+            xsend.at[slot, c, d // group],
             xrecv.at[t, c, e],
-            x_send.at[slot, c, d - base],
+            x_send.at[slot, c, d],
             x_recv.at[t, c, e],
             section,
             d,
         )
 
-    def relay_copy(t, c, j, d):
-        return remote(
-            xrelay.at[t, c, j, d // group - side * sided],
-            xrecv.at[t, c, far_base + j],
-            relay_send.at[t, c, j, d - base],
-            x_recv.at[t, c, far_base + j],
-            s,
-            d,
-        )
-
     def x_arrival(t, c, d):
         target = xrecv.at[t, c, d]
         return remote(target, target, x_send.at[0, c, 0], x_recv.at[t, c, d], s, d)
 
     def p_copy(t, c, d):
         return remote(
-            psend.at[t, c, side, d - base],
-            precv.at[t, c, own],
-            p_send.at[t, c, d - base],
-            p_recv.at[t, c, own],
-            s,
-            d,
+            psend.at[t, c, d], precv.at[t, c, e], p_send.at[t, c, d], p_recv.at[t, c, e], s, d
         )
 
     def p_arrival(t, c, d):
-        target = precv.at[t, c, d - base]
-        return remote(target, target, p_send.at[t, c, 0], p_recv.at[t, c, d - base], s, d)
+        target = precv.at[t, c, d]
+        return remote(target, target, p_send.at[t, c, 0], p_recv.at[t, c, d], s, d)
 
     def gate_send_copy(t, c):
         return remote(
-            psend.at[t, c, 1 - side],
+            psend.at[t, c, pl.ds(far_base, mid)],
             pgate.at[t, c, own],
             gate_send.at[t, c],
             gate_recv.at[t, c, own],
@@ -264,11 +244,9 @@
             ]
             for k in range(top)
         ]
+        sel[t] = sum(jnp.concatenate(blocks[k], axis=0) for k in range(top)).astype(half)
         for h in range(2):
             experts = range(h * sided, (h + 1) * sided)
-            sel[t, h] = sum(
-                jnp.concatenate([blocks[k][x] for x in experts], axis=0) for k in range(top)
-            ).astype(half)
             for k in range(top):
                 spread = jnp.concatenate(
                     [blocks[k][x] for x in experts for _ in range(group)], axis=0
@@ -288,19 +266,18 @@
 
     def pack(target, table, value):
         packed = jnp.dot(table, value, preferred_element_type=single)
-        for x in range(sided):
+        for x in range(EXPERTS):
             target[x] = packed[x * cap : (x + 1) * cap].astype(half)
 
     def dispatch(t, c):
         own_copy(t, c).wait()
-        far_copy(t, t, c, s, xown.at[t, c]).start()
-        pack(xsend.at[t, c], sel[t, side], xown[t, c])
+        pack(xsend.at[t, c], sel[t], xown[t, c])
+        far(lambda d: x_copy(t, t, c, s, d).start())
         near(lambda d: x_copy(t, t, c, s, d).start())
-        xrecv[t, c, e] = xsend[t, c, e // group - side * sided]
+        xrecv[t, c, e] = xsend[t, c, e // group]
 
     paired = sections % 2 == 0
     leads = lax.rem(s, 2) == 0
-    table_copies(0)[0].start()
     if paired:
 
         @pl.when(jnp.logical_not(leads))
@@ -310,39 +287,30 @@
     for c in range(chunks):
         dispatch(0, c)
     for t in range(ticks):
-        for copy in table_copies(t)[1 if t == 0 else 0 :]:
-            copy.start()
+        if gated[t]:
+            for copy in table_copies(t):
+                copy.start()
 
     @pl.when(has_prev)
     def _():
         for t in range(ticks - 1):
             sel_copy(t).start()
 
-    def pass_turn():
-        for c in range(chunks):
-            far_copy(0, 0, c, s, xown.at[0, c]).wait_send()
-            near(lambda d: x_copy(0, 0, c, s, d).wait_send())
-        if paired:
+    for c in range(chunks):
+        far(lambda d: x_copy(0, 0, c, s, d).wait_send())
+        near(lambda d: x_copy(0, 0, c, s, d).wait_send())
+        if paired and c == max(chunks - 2, 0):
 
             @pl.when(leads)
             def _():
                 pl.semaphore_signal(turn, inc=1, device_id=(following, e), device_id_type=MESH)
-
-    def relay(t, c):
-        for j in range(mid):
-            if c == 0:
-                table_arrival(0, t, j).wait_recv()
-            far_arrival(t, c, j).wait_recv()
-            pack(xrelay.at[t, c, j], sel_far[t, j], xraw[t, c, j])
-            near(lambda d: relay_copy(t, c, j, d).start())
-            xrecv[t, c, far_base + j] = xrelay[t, c, j, e // group - side * sided]
 
     def combine(t, c):
         near(lambda d: gate_arrival(t, c, d).wait_recv())
         for j in range(mid):
             if c == 0:
+                table_arrival(0, t, j).wait_recv()
                 table_arrival(1, t, j).wait_recv()
-                table_arrival(2, t, j).wait_recv()
             value = jnp.concatenate(
                 [pgate[t, c, d, j].astype(single) for d in range(mid)], axis=0
             ).astype(half)
@@ -362,23 +330,8 @@
     for t in range(ticks):
         gate_val = up_val = None
         squares = jnp.zeros((rows, 1), single)
-        if t == 0:
-
-            @pl.when(not_gate)
-            def _():
-                pass_turn()
-
         for c in range(chunks):
-
-            @pl.when(is_gate)
-            def _():
-                relay(t, c)
-
-            @pl.when(not_gate)
-            def _():
-                for j in range(mid):
-                    x_arrival(t, c, far_base + j).wait_recv()
-
+            far(lambda d: x_arrival(t, c, d).wait_recv())
             near(lambda d: x_arrival(t, c, d).wait_recv())
             if t == 0:
                 for copy in gate_copy(c):
@@ -400,35 +353,51 @@
         scale = lax.rsqrt(squares * (1.0 / width) + 1e-06)
         hidden = (jax.nn.silu(gate_val * scale) * (up_val * scale)).astype(half)
         if t == 0:
-
-            @pl.when(is_gate)
-            def _():
-                pass_turn()
-
             down_copy.wait()
         for c in range(chunks):
             span = pl.ds(c * cols, cols)
             value = jnp.dot(hidden, w_down[:, span], preferred_element_type=single)
             for d in range(n):
-                psend[t, c, d // mid, d % mid] = value[d * cap : (d + 1) * cap].astype(half)
-
-            @pl.when(not_gate)
-            def _():
-                gate_send_copy(t, c).start()
+                psend[t, c, d] = value[d * cap : (d + 1) * cap].astype(half)
+            if gated[t]:
+
+                @pl.when(not_gate)
+                def _():
+                    gate_send_copy(t, c).start()
+
+                @pl.when(is_gate)
+                def _():
+                    pgate[t, c, own] = psend[t, c, pl.ds(far_base, mid)]
+
+            else:
+                far(lambda d: p_copy(t, c, d).start())
+            near(lambda d: p_copy(t, c, d).start())
+            precv[t, c, e] = psend[t, c, e]
+
+        if gated[t]:
 
             @pl.when(is_gate)
             def _():
-                pgate[t, c, own] = psend[t, c, 1 - side]
-
-            near(lambda d: p_copy(t, c, d).start())
-            precv[t, c, own] = psend[t, c, side, own]
-
-        @pl.when(is_gate)
-        def _():
-            for c in range(chunks):
-                combine(t, c)
+                for c in range(chunks):
+                    combine(t, c)
+
+        for c in range(chunks):
+            near(lambda d: p_copy(t, c, d).wait_send())
+            if gated[t]:
+
+                @pl.when(not_gate)
+                def _():
+                    gate_send_copy(t, c).wait_send()
+
+            else:
+                far(lambda d: p_copy(t, c, d).wait_send())
 
         if t < ticks - 1:
+            if paired:
+
+                @pl.when(s == 1)
+                def _():
+                    pl.semaphore_signal(turn, inc=1, device_id=(previous, e), device_id_type=MESH)
 
             @pl.when(has_next)
             def _():
@@ -443,32 +412,34 @@
                     raw_copy(t - 1, c).wait_recv()
 
             near(lambda d: p_arrival(t, c, d).wait_recv())
-            f_copy(t, c, 0).wait_recv()
+            layer = xown[t, c].astype(single)
+            if gated[t]:
+                f_copy(t, c, 0).wait_recv()
+                layer = layer + frecv[t, c].astype(single)
+                sources, table = [base + j for j in range(mid)], pick[t, side]
+            else:
+                far(lambda d: p_arrival(t, c, d).wait_recv())
+                sources = list(range(n))
+                table = jnp.concatenate([pick[t, 0], pick[t, 1]], axis=1)
             value = jnp.concatenate(
-                [precv[t, c, d].astype(single) for d in range(mid)], axis=0
+                [precv[t, c, d].astype(single) for d in sources], axis=0
             ).astype(half)
-            back = jnp.dot(pick[t, side], value, preferred_element_type=single)
-            layer = xown[t, c].astype(single) + frecv[t, c].astype(single)
+            back = jnp.dot(table, value, preferred_element_type=single)
             for k in range(top):
                 layer = layer + back[k * tokens : (k + 1) * tokens] * weights[k]
             layer = layer.astype(half)
-            out[t, :, pl.ds(c * cols, cols)] = layer
+            made[t, c] = layer
+            out_copy(t, c).start()
             if t < ticks - 1:
 
                 @pl.when(has_next)
                 def _():
-                    moved[t, c] = layer
-                    far_copy(ticks + t, t + 1, c, following, moved.at[t, c]).start()
                     pack(xsend.at[ticks + t, c], sel_in[t], layer)
+                    far(lambda d: x_copy(ticks + t, t + 1, c, following, d).start())
                     near(lambda d: x_copy(ticks + t, t + 1, c, following, d).start(), True)
                     raw_copy(t, c).start()
 
         if t < ticks - 1:
-            if paired:
-
-                @pl.when(s == 1)
-                def _():
-                    pl.semaphore_signal(turn, inc=1, device_id=(previous, e), device_id_type=MESH)
 
             @pl.when(jnp.logical_not(has_prev))
             def _():
@@ -478,35 +449,33 @@
                     dispatch(t + 1, c)
 
     for t in range(ticks):
-        for copy in table_copies(t):
-            copy.wait_send()
+        if gated[t]:
+            for copy in table_copies(t):
+                copy.wait_send()
         for c in range(chunks):
-            near(lambda d: p_copy(t, c, d).wait_send())
-
-            @pl.when(not_gate)
-            def _():
-                gate_send_copy(t, c).wait_send()
-
-            @pl.when(is_gate)
-            def _():
-                for j in range(mid):
-                    f_copy(t, c, j).wait_send()
-                    near(lambda d: relay_copy(t, c, j, d).wait_send())
+            if gated[t]:
+
+                @pl.when(is_gate)
+                def _():
+                    for j in range(mid):
+                        f_copy(t, c, j).wait_send()
 
             if t > 0:
 
                 @pl.when(jnp.logical_not(has_prev))
                 def _():
-                    far_copy(t, t, c, s, xown.at[t, c]).wait_send()
+                    far(lambda d: x_copy(t, t, c, s, d).wait_send())
                     near(lambda d: x_copy(t, t, c, s, d).wait_send())
 
             if t < ticks - 1:
 
                 @pl.when(has_next)
                 def _():
-                    far_copy(ticks + t, t + 1, c, following, moved.at[t, c]).wait_send()
+                    far(lambda d: x_copy(ticks + t, t + 1, c, following, d).wait_send())
                     near(lambda d: x_copy(ticks + t, t + 1, c, following, d).wait_send(), True)
                     raw_copy(t, c).wait_send()
+
+            out_copy(t, c).wait()
 
     @pl.when(has_prev)
     def _():
@@ -524,7 +493,7 @@
         chunks = 5 if width % (5 * 128) == 0 else 4
         cols = width // chunks
         cap = min(CAP, tokens)
-        mid, sided, moves = n // 2, EXPERTS // 2, max(ticks - 1, 1)
+        mid, moves = n // 2, max(ticks - 1, 1)
         half, single = jnp.bfloat16, jnp.float32
         anywhere = pl.BlockSpec(memory_space=pl.ANY)
         vmem = pl.BlockSpec(memory_space=pltpu.VMEM)
@@ -533,44 +502,39 @@
             functools.partial(kernel, n, sections),
             out_shape=jax.ShapeDtypeStruct((ticks, tokens, width), half),
             in_specs=[anywhere, anywhere, vmem, vmem, vmem, anywhere, anywhere, anywhere],
-            out_specs=vmem,
+            out_specs=anywhere,
             scratch_shapes=[
                 pltpu.VMEM((width, hidden), half),
                 pltpu.VMEM((width, hidden), half),
                 pltpu.VMEM((hidden, width), half),
                 pltpu.VMEM((ticks, chunks, tokens, cols), half),
-                pltpu.VMEM((moves, chunks, tokens, cols), half),
-                pltpu.VMEM((2 * ticks - 1, chunks, sided, cap, cols), half),
-                pltpu.VMEM((ticks, chunks, mid, tokens, cols), half),
-                pltpu.VMEM((ticks, chunks, mid, sided, cap, cols), half),
+                pltpu.VMEM((ticks, chunks, tokens, cols), half),
+                pltpu.VMEM((2 * ticks - 1, chunks, EXPERTS, cap, cols), half),
                 pltpu.VMEM((ticks, chunks, n, cap, cols), half),
-                pltpu.VMEM((ticks, chunks, 2, mid, cap, cols), half),
-                pltpu.VMEM((ticks, chunks, mid, cap, cols), half),
+                pltpu.VMEM((ticks, chunks, n, cap, cols), half),
+                pltpu.VMEM((ticks, chunks, n, cap, cols), half),
                 pltpu.VMEM((ticks, chunks, mid, mid, cap, cols), half),
                 pltpu.VMEM((ticks, chunks, mid, tokens, cols), half),
                 pltpu.VMEM((ticks, chunks, tokens, cols), half),
-                pltpu.VMEM((ticks, 2, sided * cap, tokens), half),
-                pltpu.VMEM((moves, sided * cap, tokens), half),
-                pltpu.VMEM((ticks, mid, sided * cap, tokens), half),
+                pltpu.VMEM((ticks, EXPERTS * cap, tokens), half),
+                pltpu.VMEM((moves, EXPERTS * cap, tokens), half),
                 pltpu.VMEM((ticks, 2, top * tokens, mid * cap), half),
                 pltpu.VMEM((ticks, mid, top * tokens, mid * cap), half),
                 pltpu.VMEM((ticks, 8, 128), single),
                 pltpu.VMEM((ticks, mid, 8, 128), single),
                 dma((3, chunks)),
                 dma((ticks, chunks)),
-                dma((3, ticks)),
-                dma((3, ticks, mid)),
+                dma((ticks, chunks)),
+                dma((2, ticks)),
+                dma((2, ticks, mid)),
                 dma((moves,)),
                 dma((moves,)),
                 dma((moves, chunks)),
                 dma((moves, chunks)),
-                dma((2 * ticks - 1, chunks)),
-                dma((ticks, chunks, mid)),
-                dma((2 * ticks - 1, chunks, mid)),
+                dma((2 * ticks - 1, chunks, n)),
                 dma((ticks, chunks, n)),
-                dma((ticks, chunks, mid, mid)),
-                dma((ticks, chunks, mid)),
-                dma((ticks, chunks, mid)),
+                dma((ticks, chunks, n)),
+                dma((ticks, chunks, n)),
                 dma((ticks, chunks)),
                 dma((ticks, chunks, mid)),
                 dma((ticks, chunks, mid)),

time: 59.6 us -> 61.8 us (1.037)
  Pallas kernels: 57.7 us -> 59.9 us
    pallas_call x1, Pallas kernels: 57.7 us -> 59.9 us  [shards(): pl.pallas_call(functools.partial(kernel, n, sections), out_shape=jax.Shap...]
where the time goes in v5:
time: 61.8 us; the launch traced here: 61.6 us
  Pallas kernels  59.9 us (97%)
  local copies, waits for them, and re-layouts  1.72 us (3%)
    pallas_call x1, Pallas kernels, shards(): pl.pallas_call(functools.partial(kernel, n, sections), out_shape=jax.Shap...  59.9 us
    unnamed x1, local copies, waits for them, and re-layouts  1.72 us

profile of v5, /device:TPU:0, one launch (start us, length us, event | category | flops | bytes accessed | tf_op | source)
XLA Modules:
  0.0 61.6 jit_solution(12339033502246662148)
XLA Ops:
  0.0 59.9 %shard_map.82 = bf16[2,32,2560]{2,1,0:T(8,128)(2,1)} custom-call(bf16[32,2560]{1,0:T(8,128)(2,1)} %bitcast.13, bf16[1,32,2560]{2,1,0:T(8,128)(2,1)} %incoming.1, s32[2,1,2,32]{3,2,1,0:T(2,128)} %bitcast.14, f32[2,1,2,32]{3,2,1,0:T(2,128)} %bitcast.15, f32[1,2560]{1,0:T(1,128)} %gain.1, bf16[2560,768]{1,0:T(8,128)(2,1)} %bitcast.9, ...), custom_call_target="tpu_custom_call" | custom-call | tf_op jit(solution)/shard_map/pallas_call | solution.py:501
  59.9 1.7 %copy.11 = bf16[2,1,32,2560]{3,2,1,0:T(8,128)(2,1)} copy(bf16[2,1,32,2560]{3,2,1,0:T(8,128)(2,1)} %bitcast.12) | data formatting | bytes 655360

commit v6 on v5

--- a/solution.py
+++ b/solution.py
@@ -30,6 +30,8 @@
     xown,
     made,
     xsend,
+    xraw,
+    xrelay,
     xrecv,
     psend,
     precv,
@@ -38,6 +40,7 @@
     frecv,
     sel,
     sel_in,
+    sel_far,
     pick,
     pick_far,
     rate,
@@ -51,8 +54,11 @@
     sel_recv,
     raw_send,
     raw_recv,
+    far_send,
+    far_recv,
     x_send,
     x_recv,
+    relay_send,
     p_send,
     p_recv,
     gate_send,
@@ -70,6 +76,7 @@
     mid = n // 2
     sided = EXPERTS // 2
     gated = [t < ticks - 1 for t in range(ticks)]
+    early = max(chunks - 2, 1)
     width = chunks * cols
     rows = n * cap
     side = e // mid
@@ -105,10 +112,18 @@
 
         lax.fori_loop(0, mid, step, 0)
 
+    def sent(source, send):
+        remote(source, source, send, send, s, far_gate).wait_send()
+
+    def landed(target, recv):
+        remote(target, target, recv, recv, s, far_gate).wait_recv()
+
     def own_copy(t, c):
         source = acts if t == 0 else incoming.at[t - 1]
         return pltpu.make_async_copy(
-            source.at[:, pl.ds(c * cols, cols)], xown.at[t, c], own_sem.at[t, c]
+            source.at[:, pl.ds(c * cols, cols)],
+            xown.at[t, c],
+            own_sem.at[c if t == 0 else chunks + t - 1],
         )
 
     def gate_copy(c):
@@ -121,78 +136,84 @@
     down_copy = pltpu.make_async_copy(w_down_hbm, w_down, w_sem.at[2, 0])
 
     def table_copies(t):
-        pairs = ((pick.at[t, 1 - side], pick_far), (rate.at[t], rate_far))
+        pairs = ((sel.at[t, 1 - side], sel_far), (pick.at[t, 1 - side], pick_far), (rate.at[t], rate_far))
         return [
             remote(
-                source,
-                target.at[t, own],
-                table_send.at[i, t],
-                table_recv.at[i, t, own],
-                s,
-                far_gate,
+                source, target.at[t, own], table_send.at[i, t], table_recv.at[i, t], s, far_gate
             )
             for i, (source, target) in enumerate(pairs)
-        ]
-
-    def table_arrival(i, t, j):
-        target = (pick_far, rate_far)[i].at[t, j]
-        return remote(target, target, table_send.at[i, t], table_recv.at[i, t, j], s, far_base + j)
+        ][: 3 if gated[t] else 1]
+
+    def table_arrival(i, t):
+        landed((sel_far, pick_far, rate_far)[i].at[t], table_recv.at[i, t])
+
+    def sel_copy(t):
+        return remote(
+            sel.at[t + 1, side], sel_in.at[t], sel_send.at[t], sel_recv.at[t], previous, e
+        )
+
+    def raw_copy(t, c):
+        return remote(
+            made.at[t, c], xown.at[t + 1, c], raw_send.at[t], raw_recv.at[t], following, e
+        )
+
+    def bank(slot, c):
+        return slot if slot > 0 or c < early else 2 * ticks - 1
+
+    def far_copy(slot, t, c, section, source):
+        return remote(
+            source, xraw.at[t, c, own], far_send.at[bank(slot, c)], far_recv.at[t, c], section, far_gate
+        )
+
+    def x_copy(slot, t, c, section, d):
+        return remote(
+            xsend.at[slot, c, d // group - side * sided],
+            xrecv.at[t, c, e],
+            x_send.at[bank(slot, c)],
+            x_recv.at[t, c],
+            section,
+            d,
+        )
+
+    def dispatched(slot, first, last, peers):
+        span = pl.ds(first, last - first)
+        sent(xown.at[0, span], far_send.at[bank(slot, first)])
+        if peers:
+            sent(xrecv.at[0, span, pl.ds(0, peers)], x_send.at[bank(slot, first)])
+
+    def relay_copy(t, c, j, d):
+        return remote(
+            xrelay.at[t, c, j, d // group - side * sided],
+            xrecv.at[t, c, far_base + j],
+            relay_send.at[t, j],
+            x_recv.at[t, c],
+            s,
+            d,
+        )
+
+    def p_copy(t, c, d):
+        return remote(
+            psend.at[t, c, d], precv.at[t, c, e], p_send.at[t], p_recv.at[t, c], s, d
+        )
+
+    def gate_send_copy(t, c):
+        return remote(
+            psend.at[t, c, pl.ds(far_base, mid)],
+            pgate.at[t, c, own],
+            gate_send.at[t],
+            gate_recv.at[t, c],
+            s,
+            near_gate,
+        )
+
+    def f_copy(t, c, j):
+        return remote(
+            fsend.at[t, c, j], frecv.at[t, c], f_send.at[t], f_recv.at[t, c], s, far_base + j
+        )
 
     def out_copy(t, c):
         return pltpu.make_async_copy(
-            made.at[t, c], out.at[t, :, pl.ds(c * cols, cols)], out_sem.at[t, c]
-        )
-
-    def sel_copy(t):
-        return remote(
-            sel.at[t + 1], sel_in.at[t], sel_send.at[t], sel_recv.at[t], previous, e
-        )
-
-    def raw_copy(t, c):
-        return remote(
-            made.at[t, c], xown.at[t + 1, c], raw_send.at[t, c], raw_recv.at[t, c], following, e
-        )
-
-    def x_copy(slot, t, c, section, d):
-        return remote(
-            xsend.at[slot, c, d // group],
-            xrecv.at[t, c, e],
-            x_send.at[slot, c, d],
-            x_recv.at[t, c, e],
-            section,
-            d,
-        )
-
-    def x_arrival(t, c, d):
-        target = xrecv.at[t, c, d]
-        return remote(target, target, x_send.at[0, c, 0], x_recv.at[t, c, d], s, d)
-
-    def p_copy(t, c, d):
-        return remote(
-            psend.at[t, c, d], precv.at[t, c, e], p_send.at[t, c, d], p_recv.at[t, c, e], s, d
-        )
-
-    def p_arrival(t, c, d):
-        target = precv.at[t, c, d]
-        return remote(target, target, p_send.at[t, c, 0], p_recv.at[t, c, d], s, d)
-
-    def gate_send_copy(t, c):
-        return remote(
-            psend.at[t, c, pl.ds(far_base, mid)],
-            pgate.at[t, c, own],
-            gate_send.at[t, c],
-            gate_recv.at[t, c, own],
-            s,
-            near_gate,
-        )
-
-    def gate_arrival(t, c, d):
-        target = pgate.at[t, c, d - base]
-        return remote(target, target, gate_send.at[t, c], gate_recv.at[t, c, d - base], s, d)
-
-    def f_copy(t, c, j):
-        return remote(
-            fsend.at[t, c, j], frecv.at[t, c], f_send.at[t, c, j], f_recv.at[t, c], s, far_base + j
+            made.at[t, c], out.at[t, :, pl.ds(c * cols, cols)], out_sem.at[0]
         )
 
     for c in range(chunks):
@@ -244,9 +265,11 @@
             ]
             for k in range(top)
         ]
-        sel[t] = sum(jnp.concatenate(blocks[k], axis=0) for k in range(top)).astype(half)
         for h in range(2):
             experts = range(h * sided, (h + 1) * sided)
+            sel[t, h] = sum(
+                jnp.concatenate([blocks[k][x] for x in experts], axis=0) for k in range(top)
+            ).astype(half)
             for k in range(top):
                 spread = jnp.concatenate(
                     [blocks[k][x] for x in experts for _ in range(group)], axis=0
@@ -266,18 +289,23 @@
 
     def pack(target, table, value):
         packed = jnp.dot(table, value, preferred_element_type=single)
-        for x in range(EXPERTS):
+        for x in range(sided):
             target[x] = packed[x * cap : (x + 1) * cap].astype(half)
 
+    def landed_own(t):
+        pltpu.make_async_copy(xown.at[t], xown.at[t], own_sem.at[chunks + t - 1]).wait()
+
     def dispatch(t, c):
-        own_copy(t, c).wait()
-        pack(xsend.at[t, c], sel[t], xown[t, c])
-        far(lambda d: x_copy(t, t, c, s, d).start())
+        if t == 0:
+            own_copy(t, c).wait()
+        far_copy(t, t, c, s, xown.at[t, c]).start()
+        pack(xsend.at[t, c], sel[t, side], xown[t, c])
         near(lambda d: x_copy(t, t, c, s, d).start())
-        xrecv[t, c, e] = xsend[t, c, e // group]
+        xrecv[t, c, e] = xsend[t, c, e // group - side * sided]
 
     paired = sections % 2 == 0
     leads = lax.rem(s, 2) == 0
+    table_copies(0)[0].start()
     if paired:
 
         @pl.when(jnp.logical_not(leads))
@@ -287,30 +315,37 @@
     for c in range(chunks):
         dispatch(0, c)
     for t in range(ticks):
-        if gated[t]:
-            for copy in table_copies(t):
-                copy.start()
+        for copy in table_copies(t)[1 if t == 0 else 0 :]:
+            copy.start()
 
     @pl.when(has_prev)
     def _():
         for t in range(ticks - 1):
             sel_copy(t).start()
 
-    for c in range(chunks):
-        far(lambda d: x_copy(0, 0, c, s, d).wait_send())
-        near(lambda d: x_copy(0, 0, c, s, d).wait_send())
-        if paired and c == max(chunks - 2, 0):
-
-            @pl.when(leads)
-            def _():
-                pl.semaphore_signal(turn, inc=1, device_id=(following, e), device_id_type=MESH)
+    dispatched(0, 0, early, mid - 1)
+    if paired:
+
+        @pl.when(leads)
+        def _():
+            pl.semaphore_signal(turn, inc=1, device_id=(following, e), device_id_type=MESH)
+
+    def relay(t, c):
+        if c == 0:
+            table_arrival(0, t)
+        landed(xraw.at[t, c], far_recv.at[t, c])
+        for j in range(mid):
+            pack(xrelay.at[t, c, j], sel_far[t, j], xraw[t, c, j])
+            near(lambda d: relay_copy(t, c, j, d).start())
+            xrecv[t, c, far_base + j] = xrelay[t, c, j, e // group - side * sided]
 
     def combine(t, c):
-        near(lambda d: gate_arrival(t, c, d).wait_recv())
+        if c == 0:
+            table_arrival(1, t)
+            table_arrival(2, t)
+        if mid > 1:
+            landed(pgate.at[t, c, pl.ds(0, mid - 1)], gate_recv.at[t, c])
         for j in range(mid):
-            if c == 0:
-                table_arrival(0, t, j).wait_recv()
-                table_arrival(1, t, j).wait_recv()
             value = jnp.concatenate(
                 [pgate[t, c, d, j].astype(single) for d in range(mid)], axis=0
             ).astype(half)
@@ -331,17 +366,29 @@
         gate_val = up_val = None
         squares = jnp.zeros((rows, 1), single)
         for c in range(chunks):
-            far(lambda d: x_arrival(t, c, d).wait_recv())
-            near(lambda d: x_arrival(t, c, d).wait_recv())
+
+            @pl.when(jnp.logical_and(is_gate, leads) if paired and t > 0 else is_gate)
+            def _():
+                relay(t, c)
+
+            for packed, there in ((0, is_gate), (mid, not_gate)):
+                if t == 0:
+                    cases = ((mid - 1, there),)
+                else:
+                    cases = (
+                        (mid, jnp.logical_and(there, has_prev)),
+                        (mid - 1, jnp.logical_and(there, jnp.logical_not(has_prev))),
+                    )
+                for number, case in cases:
+                    if packed + number:
+
+                        @pl.when(case)
+                        def _():
+                            landed(xrecv.at[t, c, pl.ds(0, packed + number)], x_recv.at[t, c])
+
             if t == 0:
                 for copy in gate_copy(c):
                     copy.wait()
-            else:
-
-                @pl.when(has_prev)
-                def _():
-                    x_arrival(t, c, e).wait_recv()
-
             span = pl.ds(c * cols, cols)
             value = jnp.concatenate([xrecv[t, c, d].astype(single) for d in range(n)], axis=0)
             squares = squares + jnp.sum(value * value, axis=1, keepdims=True)
@@ -381,16 +428,17 @@
                 for c in range(chunks):
                     combine(t, c)
 
-        for c in range(chunks):
-            near(lambda d: p_copy(t, c, d).wait_send())
-            if gated[t]:
-
-                @pl.when(not_gate)
-                def _():
-                    gate_send_copy(t, c).wait_send()
-
-            else:
-                far(lambda d: p_copy(t, c, d).wait_send())
+        if gated[t]:
+
+            @pl.when(not_gate)
+            def _():
+                sent(psend.at[t, :, pl.ds(0, mid)], gate_send.at[t])
+
+            peers = mid - 1
+        else:
+            peers = n - 1
+        if peers:
+            sent(psend.at[t, :, pl.ds(0, peers)], p_send.at[t])
 
         if t < ticks - 1:
             if paired:
@@ -399,28 +447,33 @@
                 def _():
                     pl.semaphore_signal(turn, inc=1, device_id=(previous, e), device_id_type=MESH)
 
+                @pl.when(jnp.logical_and(is_gate, jnp.logical_not(leads)))
+                def _():
+                    for c in range(chunks):
+                        relay(t + 1, c)
+
             @pl.when(has_next)
             def _():
-                sel_copy(t).wait_recv()
+                landed(sel_in.at[t], sel_recv.at[t])
+
+        if t > 0:
+
+            @pl.when(has_prev)
+            def _():
+                landed(xown.at[t], raw_recv.at[t - 1])
 
         weights = [column(rate[t], k) for k in range(top)]
         for c in range(chunks):
-            if t > 0:
-
-                @pl.when(has_prev)
-                def _():
-                    raw_copy(t - 1, c).wait_recv()
-
-            near(lambda d: p_arrival(t, c, d).wait_recv())
             layer = xown[t, c].astype(single)
             if gated[t]:
-                f_copy(t, c, 0).wait_recv()
+                landed(frecv.at[t, c], f_recv.at[t, c])
                 layer = layer + frecv[t, c].astype(single)
                 sources, table = [base + j for j in range(mid)], pick[t, side]
             else:
-                far(lambda d: p_arrival(t, c, d).wait_recv())
                 sources = list(range(n))
                 table = jnp.concatenate([pick[t, 0], pick[t, 1]], axis=1)
+            if peers:
+                landed(precv.at[t, c, pl.ds(0, peers)], p_recv.at[t, c])
             value = jnp.concatenate(
                 [precv[t, c, d].astype(single) for d in sources], axis=0
             ).astype(half)
@@ -434,8 +487,8 @@
 
                 @pl.when(has_next)
                 def _():
+                    far_copy(ticks + t, t + 1, c, following, made.at[t, c]).start()
                     pack(xsend.at[ticks + t, c], sel_in[t], layer)
-                    far(lambda d: x_copy(ticks + t, t + 1, c, following, d).start())
                     near(lambda d: x_copy(ticks + t, t + 1, c, following, d).start(), True)
                     raw_copy(t, c).start()
 
@@ -445,37 +498,37 @@
             def _():
                 if paired:
                     pl.semaphore_wait(turn, 1)
+                landed_own(t + 1)
                 for c in range(chunks):
                     dispatch(t + 1, c)
 
+    dispatched(0, early, chunks, mid - 1)
     for t in range(ticks):
-        if gated[t]:
-            for copy in table_copies(t):
-                copy.wait_send()
-        for c in range(chunks):
+        for copy in table_copies(t):
+            copy.wait_send()
+
+        @pl.when(is_gate)
+        def _():
+            if mid > 1:
+                for j in range(mid):
+                    sent(xrecv.at[t, :, pl.ds(0, mid - 1)], relay_send.at[t, j])
             if gated[t]:
-
-                @pl.when(is_gate)
-                def _():
-                    for j in range(mid):
-                        f_copy(t, c, j).wait_send()
-
-            if t > 0:
-
-                @pl.when(jnp.logical_not(has_prev))
-                def _():
-                    far(lambda d: x_copy(t, t, c, s, d).wait_send())
-                    near(lambda d: x_copy(t, t, c, s, d).wait_send())
-
-            if t < ticks - 1:
-
-                @pl.when(has_next)
-                def _():
-                    far(lambda d: x_copy(ticks + t, t + 1, c, following, d).wait_send())
-                    near(lambda d: x_copy(ticks + t, t + 1, c, following, d).wait_send(), True)
-                    raw_copy(t, c).wait_send()
-
-            out_copy(t, c).wait()
+                sent(fsend.at[t], f_send.at[t])
+
+        if t > 0:
+
+            @pl.when(jnp.logical_not(has_prev))
+            def _():
+                dispatched(t, 0, chunks, mid - 1)
+
+        if t < ticks - 1:
+
+            @pl.when(has_next)
+            def _():
+                dispatched(ticks + t, 0, chunks, mid)
+                sent(made.at[t], raw_send.at[t])
+
+    pltpu.make_async_copy(made, made, out_sem.at[0]).wait()
 
     @pl.when(has_prev)
     def _():
@@ -493,7 +546,7 @@
         chunks = 5 if width % (5 * 128) == 0 else 4
         cols = width // chunks
         cap = min(CAP, tokens)
-        mid, moves = n // 2, max(ticks - 1, 1)
+        mid, sided, moves = n // 2, EXPERTS // 2, max(ticks - 1, 1)
         half, single = jnp.bfloat16, jnp.float32
         anywhere = pl.BlockSpec(memory_space=pl.ANY)
         vmem = pl.BlockSpec(memory_space=pltpu.VMEM)
@@ -509,36 +562,42 @@
                 pltpu.VMEM((hidden, width), half),
                 pltpu.VMEM((ticks, chunks, tokens, cols), half),
                 pltpu.VMEM((ticks, chunks, tokens, cols), half),
-                pltpu.VMEM((2 * ticks - 1, chunks, EXPERTS, cap, cols), half),
+                pltpu.VMEM((2 * ticks - 1, chunks, sided, cap, cols), half),
+                pltpu.VMEM((ticks, chunks, mid, tokens, cols), half),
+                pltpu.VMEM((ticks, chunks, mid, sided, cap, cols), half),
                 pltpu.VMEM((ticks, chunks, n, cap, cols), half),
                 pltpu.VMEM((ticks, chunks, n, cap, cols), half),
                 pltpu.VMEM((ticks, chunks, n, cap, cols), half),
-                pltpu.VMEM((ticks, chunks, mid, mid, cap, cols), half),
-                pltpu.VMEM((ticks, chunks, mid, tokens, cols), half),
-                pltpu.VMEM((ticks, chunks, tokens, cols), half),
-                pltpu.VMEM((ticks, EXPERTS * cap, tokens), half),
-                pltpu.VMEM((moves, EXPERTS * cap, tokens), half),
+                pltpu.VMEM((moves, chunks, mid, mid, cap, cols), half),
+                pltpu.VMEM((moves, chunks, mid, tokens, cols), half),
+                pltpu.VMEM((moves, chunks, tokens, cols), half),
+                pltpu.VMEM((ticks, 2, sided * cap, tokens), half),
+                pltpu.VMEM((moves, sided * cap, tokens), half),
+                pltpu.VMEM((ticks, mid, sided * cap, tokens), half),
                 pltpu.VMEM((ticks, 2, top * tokens, mid * cap), half),
                 pltpu.VMEM((ticks, mid, top * tokens, mid * cap), half),
                 pltpu.VMEM((ticks, 8, 128), single),
                 pltpu.VMEM((ticks, mid, 8, 128), single),
                 dma((3, chunks)),
-                dma((ticks, chunks)),
-                dma((ticks, chunks)),
-                dma((2, ticks)),
-                dma((2, ticks, mid)),
+                dma((1,)),
+                dma((chunks + moves,)),
+                dma((3, ticks)),
+                dma((3, ticks)),
                 dma((moves,)),
                 dma((moves,)),
+                dma((moves,)),
+                dma((moves,)),
+                dma((2 * ticks,)),
+                dma((ticks, chunks)),
+                dma((2 * ticks,)),
+                dma((ticks, chunks)),
+                dma((ticks, mid)),
+                dma((ticks,)),
+                dma((ticks, chunks)),
+                dma((moves,)),
                 dma((moves, chunks)),
+                dma((moves,)),
                 dma((moves, chunks)),
-                dma((2 * ticks - 1, chunks, n)),
-                dma((ticks, chunks, n)),
-                dma((ticks, chunks, n)),
-                dma((ticks, chunks, n)),
-                dma((ticks, chunks)),
-                dma((ticks, chunks, mid)),
-                dma((ticks, chunks, mid)),
-                dma((ticks, chunks)),
                 pltpu.SemaphoreType.REGULAR,
             ],
             compiler_params=pltpu.CompilerParams(

time: 61.8 us -> 58.4 us (0.945)
  Pallas kernels: 59.9 us -> 56.5 us
    pallas_call x1, Pallas kernels: 59.9 us -> 56.5 us  [shards(): pl.pallas_call(functools.partial(kernel, n, sections), out_shape=jax.Shap...]
where the time goes in v6:
time: 58.4 us; the launch traced here: 58.2 us
  Pallas kernels  56.5 us (97%)
  local copies, waits for them, and re-layouts  1.72 us (3%)
    pallas_call x1, Pallas kernels, shards(): pl.pallas_call(functools.partial(kernel, n, sections), out_shape=jax.Shap...  56.5 us
    unnamed x1, local copies, waits for them, and re-layouts  1.72 us

profile of v6, /device:TPU:0, one launch (start us, length us, event | category | flops | bytes accessed | tf_op | source)
XLA Modules:
  0.0 58.2 jit_solution(15935486761315425535)
XLA Ops:
  0.0 56.5 %shard_map.82 = bf16[2,32,2560]{2,1,0:T(8,128)(2,1)} custom-call(bf16[32,2560]{1,0:T(8,128)(2,1)} %bitcast.13, bf16[1,32,2560]{2,1,0:T(8,128)(2,1)} %incoming.1, s32[2,1,2,32]{3,2,1,0:T(2,128)} %bitcast.14, f32[2,1,2,32]{3,2,1,0:T(2,128)} %bitcast.15, f32[1,2560]{1,0:T(1,128)} %gain.1, bf16[2560,768]{1,0:T(8,128)(2,1)} %bitcast.9, ...), custom_call_target="tpu_custom_call" | custom-call | tf_op jit(solution)/shard_map/pallas_call | solution.py:554
  56.5 1.7 %copy.11 = bf16[2,1,32,2560]{3,2,1,0:T(8,128)(2,1)} copy(bf16[2,1,32,2560]{3,2,1,0:T(8,128)(2,1)} %bitcast.12) | data formatting | bytes 655360

commit v7 on v6

--- a/solution.py
+++ b/solution.py
@@ -17,13 +17,16 @@
     sections,
     acts,
     incoming,
-    routes,
-    route_weight,
-    gain,
+    routes_hbm,
+    route_weight_hbm,
+    gain_hbm,
     w_gate_hbm,
     w_up_hbm,
     w_down_hbm,
     out,
+    routes,
+    route_weight,
+    gain,
     w_gate,
     w_up,
     w_down,
@@ -45,6 +48,7 @@
     pick_far,
     rate,
     rate_far,
+    small_sem,
     w_sem,
     out_sem,
     own_sem,
@@ -216,6 +220,14 @@
             made.at[t, c], out.at[t, :, pl.ds(c * cols, cols)], out_sem.at[0]
         )
 
+    small = [
+        pltpu.make_async_copy(source, target, small_sem.at[i])
+        for i, (source, target) in enumerate(
+            ((routes_hbm, routes), (route_weight_hbm, route_weight), (gain_hbm, gain))
+        )
+    ]
+    for copy in small:
+        copy.start()
     for c in range(chunks):
         own_copy(0, c).start()
 
@@ -245,6 +257,9 @@
         for t in range(1, ticks):
             for c in range(chunks):
                 own_copy(t, c).start()
+
+    for copy in small:
+        copy.wait()
 
     def iota(shape, axis):
         return lax.broadcasted_iota(jnp.int32, shape, axis)
@@ -305,6 +320,7 @@
 
     paired = sections % 2 == 0
     leads = lax.rem(s, 2) == 0
+    held = leads if paired else s < 0
     table_copies(0)[0].start()
     if paired:
 
@@ -357,6 +373,12 @@
             fsend[t, c, j] = total.astype(half)
             f_copy(t, c, j).start()
 
+    def forward(t, c):
+        far_copy(ticks + t, t + 1, c, following, made.at[t, c]).start()
+        pack(xsend.at[ticks + t, c], sel_in[t], made[t, c])
+        near(lambda d: x_copy(ticks + t, t + 1, c, following, d).start(), True)
+        raw_copy(t, c).start()
+
     def column(table, k):
         return jnp.sum(
             jnp.where(diagonal, table[k : k + 1, 0:tokens], 0.0), axis=1, keepdims=True
@@ -367,7 +389,7 @@
         squares = jnp.zeros((rows, 1), single)
         for c in range(chunks):
 
-            @pl.when(jnp.logical_and(is_gate, leads) if paired and t > 0 else is_gate)
+            @pl.when(is_gate)
             def _():
                 relay(t, c)
 
@@ -434,6 +456,10 @@
             def _():
                 sent(psend.at[t, :, pl.ds(0, mid)], gate_send.at[t])
 
+            @pl.when(is_gate)
+            def _():
+                sent(fsend.at[t], f_send.at[t])
+
             peers = mid - 1
         else:
             peers = n - 1
@@ -443,14 +469,9 @@
         if t < ticks - 1:
             if paired:
 
-                @pl.when(s == 1)
+                @pl.when(jnp.logical_not(leads))
                 def _():
                     pl.semaphore_signal(turn, inc=1, device_id=(previous, e), device_id_type=MESH)
-
-                @pl.when(jnp.logical_and(is_gate, jnp.logical_not(leads)))
-                def _():
-                    for c in range(chunks):
-                        relay(t + 1, c)
 
             @pl.when(has_next)
             def _():
@@ -485,19 +506,22 @@
             out_copy(t, c).start()
             if t < ticks - 1:
 
-                @pl.when(has_next)
+                @pl.when(jnp.logical_and(has_next, jnp.logical_not(held)))
                 def _():
-                    far_copy(ticks + t, t + 1, c, following, made.at[t, c]).start()
-                    pack(xsend.at[ticks + t, c], sel_in[t], layer)
-                    near(lambda d: x_copy(ticks + t, t + 1, c, following, d).start(), True)
-                    raw_copy(t, c).start()
+                    forward(t, c)
+
+        if t < ticks - 1 and paired:
+
+            @pl.when(held)
+            def _():
+                pl.semaphore_wait(turn, 1)
+                for c in range(chunks):
+                    forward(t, c)
 
         if t < ticks - 1:
 
             @pl.when(jnp.logical_not(has_prev))
             def _():
-                if paired:
-                    pl.semaphore_wait(turn, 1)
                 landed_own(t + 1)
                 for c in range(chunks):
                     dispatch(t + 1, c)
@@ -512,8 +536,6 @@
             if mid > 1:
                 for j in range(mid):
                     sent(xrecv.at[t, :, pl.ds(0, mid - 1)], relay_send.at[t, j])
-            if gated[t]:
-                sent(fsend.at[t], f_send.at[t])
 
         if t > 0:
 
@@ -549,14 +571,16 @@
         mid, sided, moves = n // 2, EXPERTS // 2, max(ticks - 1, 1)
         half, single = jnp.bfloat16, jnp.float32
         anywhere = pl.BlockSpec(memory_space=pl.ANY)
-        vmem = pl.BlockSpec(memory_space=pltpu.VMEM)
         dma = pltpu.SemaphoreType.DMA
         result = pl.pallas_call(
             functools.partial(kernel, n, sections),
             out_shape=jax.ShapeDtypeStruct((ticks, tokens, width), half),
-            in_specs=[anywhere, anywhere, vmem, vmem, vmem, anywhere, anywhere, anywhere],
+            in_specs=[anywhere] * 8,
             out_specs=anywhere,
             scratch_shapes=[
+                pltpu.VMEM((ticks, 1, top, tokens), routes.dtype),
+                pltpu.VMEM((ticks, 1, top, tokens), single),
+                pltpu.VMEM(norm_gain.shape, single),
                 pltpu.VMEM((width, hidden), half),
                 pltpu.VMEM((width, hidden), half),
                 pltpu.VMEM((hidden, width), half),
@@ -578,6 +602,7 @@
                 pltpu.VMEM((ticks, mid, top * tokens, mid * cap), half),
                 pltpu.VMEM((ticks, 8, 128), single),
                 pltpu.VMEM((ticks, mid, 8, 128), single),
+                dma((3,)),
                 dma((3, chunks)),
                 dma((1,)),
                 dma((chunks + moves,)),

time: 58.4 us -> 60.5 us (1.036)
  Pallas kernels: 56.5 us -> 58.6 us
    pallas_call x1, Pallas kernels: 56.5 us -> 58.6 us  [shards(): pl.pallas_call(functools.partial(kernel, n, sections), out_shape=jax.Shap...]
where the time goes in v7:
time: 60.5 us; the launch traced here: 60.3 us
  Pallas kernels  58.6 us (97%)
  local copies, waits for them, and re-layouts  1.72 us (3%)
    pallas_call x1, Pallas kernels, shards(): pl.pallas_call(functools.partial(kernel, n, sections), out_shape=jax.Shap...  58.6 us
    unnamed x1, local copies, waits for them, and re-layouts  1.72 us

profile of v7, /device:TPU:0, one launch (start us, length us, event | category | flops | bytes accessed | tf_op | source)
XLA Modules:
  0.0 60.3 jit_solution(908137564732771872)
XLA Ops:
  0.0 58.6 %shard_map.82 = bf16[2,32,2560]{2,1,0:T(8,128)(2,1)} custom-call(bf16[32,2560]{1,0:T(8,128)(2,1)} %bitcast.13, bf16[1,32,2560]{2,1,0:T(8,128)(2,1)} %incoming.1, s32[2,1,2,32]{3,2,1,0:T(2,128)} %bitcast.14, f32[2,1,2,32]{3,2,1,0:T(2,128)} %bitcast.15, f32[1,2560]{1,0:T(1,128)} %gain_hbm.1, bf16[2560,768]{1,0:T(8,128)(2,1)} %bitcast.9, ...), custom_call_target="tpu_custom_call" | custom-call | tf_op jit(solution)/shard_map/pallas_call | solution.py:575
  58.6 1.7 %copy.11 = bf16[2,1,32,2560]{3,2,1,0:T(8,128)(2,1)} copy(bf16[2,1,32,2560]{3,2,1,0:T(8,128)(2,1)} %bitcast.12) | data formatting | bytes 655360

commit v8 on v7

--- a/solution.py
+++ b/solution.py
@@ -423,6 +423,15 @@
         hidden = (jax.nn.silu(gate_val * scale) * (up_val * scale)).astype(half)
         if t == 0:
             down_copy.wait()
+
+        if t < ticks - 1:
+
+            @pl.when(jnp.logical_not(has_prev))
+            def _():
+                landed_own(t + 1)
+                for c in range(chunks):
+                    dispatch(t + 1, c)
+
         for c in range(chunks):
             span = pl.ds(c * cols, cols)
             value = jnp.dot(hidden, w_down[:, span], preferred_element_type=single)
@@ -510,21 +519,16 @@
                 def _():
                     forward(t, c)
 
-        if t < ticks - 1 and paired:
+        if t < ticks - 1:
 
             @pl.when(held)
             def _():
                 pl.semaphore_wait(turn, 1)
+
+            @pl.when(held)
+            def _():
                 for c in range(chunks):
                     forward(t, c)
-
-        if t < ticks - 1:
-
-            @pl.when(jnp.logical_not(has_prev))
-            def _():
-                landed_own(t + 1)
-                for c in range(chunks):
-                    dispatch(t + 1, c)
 
     dispatched(0, early, chunks, mid - 1)
     for t in range(ticks):

time: 60.5 us -> 55.9 us (0.924)
  the two profiles are of different devices: /device:TPU:0 before, /device:TPU:1 now
where the time goes in v8:
time: 55.9 us; the launch traced here: 55.8 us
  Pallas kernels  54.1 us (97%)
  local copies, waits for them, and re-layouts  1.72 us (3%)
    pallas_call x1, Pallas kernels, shards(): pl.pallas_call(functools.partial(kernel, n, sections), out_shape=jax.Shap...  54.1 us
    unnamed x1, local copies, waits for them, and re-layouts  1.72 us

profile of v8, /device:TPU:1, one launch (start us, length us, event | category | flops | bytes accessed | tf_op | source)
XLA Modules:
  0.0 55.8 jit_solution(7452460921039225599)
XLA Ops:
  0.0 54.1 %shard_map.82 = bf16[2,32,2560]{2,1,0:T(8,128)(2,1)} custom-call(bf16[32,2560]{1,0:T(8,128)(2,1)} %bitcast.13, bf16[1,32,2560]{2,1,0:T(8,128)(2,1)} %incoming.1, s32[2,1,2,32]{3,2,1,0:T(2,128)} %bitcast.14, f32[2,1,2,32]{3,2,1,0:T(2,128)} %bitcast.15, f32[1,2560]{1,0:T(1,128)} %gain_hbm.1, bf16[2560,768]{1,0:T(8,128)(2,1)} %bitcast.9, ...), custom_call_target="tpu_custom_call" | custom-call | tf_op jit(solution)/shard_map/pallas_call | solution.py:579
  54.1 1.7 %copy.11 = bf16[2,1,32,2560]{3,2,1,0:T(8,128)(2,1)} copy(bf16[2,1,32,2560]{3,2,1,0:T(8,128)(2,1)} %bitcast.12) | data formatting | bytes 655360

commit v9 on v8

--- a/solution.py
+++ b/solution.py
@@ -424,14 +424,6 @@
         if t == 0:
             down_copy.wait()
 
-        if t < ticks - 1:
-
-            @pl.when(jnp.logical_not(has_prev))
-            def _():
-                landed_own(t + 1)
-                for c in range(chunks):
-                    dispatch(t + 1, c)
-
         for c in range(chunks):
             span = pl.ds(c * cols, cols)
             value = jnp.dot(hidden, w_down[:, span], preferred_element_type=single)
@@ -451,6 +443,14 @@
                 far(lambda d: p_copy(t, c, d).start())
             near(lambda d: p_copy(t, c, d).start())
             precv[t, c, e] = psend[t, c, e]
+
+        if t < ticks - 1:
+
+            @pl.when(jnp.logical_not(has_prev))
+            def _():
+                landed_own(t + 1)
+                for c in range(chunks):
+                    dispatch(t + 1, c)
 
         if gated[t]:
 
@@ -630,17 +630,22 @@
                 pltpu.SemaphoreType.REGULAR,
             ],
             compiler_params=pltpu.CompilerParams(
-                collective_id=0, has_side_effects=True, vmem_limit_bytes=60 << 20
+                collective_id=0, has_side_effects=True, vmem_limit_bytes=34 << 20
             ),
         )(
-            acts[0],
-            incoming,
-            jnp.swapaxes(routes, 2, 3),
-            jnp.swapaxes(route_weight, 2, 3),
-            norm_gain,
-            w_gate[0],
-            w_up[0],
-            w_down[0],
+            *(
+                pltpu.with_memory_space_constraint(value, pltpu.HBM)
+                for value in (
+                    acts[0],
+                    incoming,
+                    jnp.swapaxes(routes, 2, 3),
+                    jnp.swapaxes(route_weight, 2, 3),
+                    norm_gain,
+                    w_gate[0],
+                    w_up[0],
+                    w_down[0],
+                )
+            )
         )
         return result[:, None]
 

time: 55.9 us -> 56 us (level)
  Pallas kernels: 54.1 us -> 55.1 us
  local copies, waits for them, and re-layouts: 1.72 us -> 0.73 us
    pallas_call x1, Pallas kernels: 54.1 us -> 55.1 us  [shards(): pl.pallas_call(functools.partial(kernel, n, sections), out_shape=jax.Shap...]
    unnamed x1, local copies, waits for them, and re-layouts: 1.72 us -> 0.73 us
where the time goes in v9:
time: 56 us; the launch traced here: 55.8 us
  Pallas kernels  55.1 us (98%)
  local copies, waits for them, and re-layouts  0.73 us (1%)
    pallas_call x1, Pallas kernels, shards(): pl.pallas_call(functools.partial(kernel, n, sections), out_shape=jax.Shap...  55.1 us

profile of v9, /device:TPU:1, one launch (start us, length us, event | category | flops | bytes accessed | tf_op | source)
XLA Modules:
  0.0 55.8 jit_solution(11660822247220042296)
XLA Ops:
  0.0 55.1 %shard_map.82 = bf16[2,32,2560]{2,1,0:T(8,128)(2,1)S(1)} custom-call(bf16[32,2560]{1,0:T(8,128)(2,1)} %bitcast.13, bf16[1,32,2560]{2,1,0:T(8,128)(2,1)} %incoming.1, s32[2,1,2,32]{3,2,1,0:T(2,128)} %bitcast.14, f32[2,1,2,32]{3,2,1,0:T(2,128)} %bitcast.15, f32[1,2560]{1,0:T(1,128)} %gain_hbm.1, bf16[2560,768]{1,0:T(8,128)(2,1)} %bitcast.10, ...), custom_call_target="tpu_custom_call" | custom-call | tf_op jit(solution)/shard_map/pallas_call | solution.py:579
  55.1 0.7 %copy.11 = bf16[2,1,32,2560]{3,2,1,0:T(8,128)(2,1)} copy(bf16[2,1,32,2560]{3,2,1,0:T(8,128)(2,1)S(1)} %bitcast.9) | data formatting | bytes 655360

commit v10 on v9

--- a/solution.py
+++ b/solution.py
@@ -389,7 +389,7 @@
         squares = jnp.zeros((rows, 1), single)
         for c in range(chunks):
 
-            @pl.when(is_gate)
+            @pl.when(is_gate if t == 0 else jnp.logical_and(is_gate, has_prev))
             def _():
                 relay(t, c)
 
@@ -520,6 +520,11 @@
                     forward(t, c)
 
         if t < ticks - 1:
+
+            @pl.when(jnp.logical_and(is_gate, jnp.logical_not(has_prev)))
+            def _():
+                for c in range(chunks):
+                    relay(t + 1, c)
 
             @pl.when(held)
             def _():

time: 56 us -> 53.1 us (0.948)
  Pallas kernels: 55.1 us -> 52.2 us
    pallas_call x1, Pallas kernels: 55.1 us -> 52.2 us  [shards(): pl.pallas_call(functools.partial(kernel, n, sections), out_shape=jax.Shap...]
where the time goes in v10:
time: 53.1 us; the launch traced here: 53 us
  Pallas kernels  52.2 us (98%)
  local copies, waits for them, and re-layouts  0.73 us (1%)
    pallas_call x1, Pallas kernels, shards(): pl.pallas_call(functools.partial(kernel, n, sections), out_shape=jax.Shap...  52.2 us

profile of v10, /device:TPU:1, one launch (start us, length us, event | category | flops | bytes accessed | tf_op | source)
XLA Modules:
  0.0 53.0 jit_solution(2717520717317369325)
XLA Ops:
  0.0 52.2 %shard_map.82 = bf16[2,32,2560]{2,1,0:T(8,128)(2,1)S(1)} custom-call(bf16[32,2560]{1,0:T(8,128)(2,1)} %bitcast.13, bf16[1,32,2560]{2,1,0:T(8,128)(2,1)} %incoming.1, s32[2,1,2,32]{3,2,1,0:T(2,128)} %bitcast.14, f32[2,1,2,32]{3,2,1,0:T(2,128)} %bitcast.15, f32[1,2560]{1,0:T(1,128)} %gain_hbm.1, bf16[2560,768]{1,0:T(8,128)(2,1)} %bitcast.10, ...), custom_call_target="tpu_custom_call" | custom-call | tf_op jit(solution)/shard_map/pallas_call | solution.py:584
  52.2 0.7 %copy.11 = bf16[2,1,32,2560]{3,2,1,0:T(8,128)(2,1)} copy(bf16[2,1,32,2560]{3,2,1,0:T(8,128)(2,1)S(1)} %bitcast.9) | data formatting | bytes 655360

commit v11 on v10

--- a/solution.py
+++ b/solution.py
@@ -80,7 +80,7 @@
     mid = n // 2
     sided = EXPERTS // 2
     gated = [t < ticks - 1 for t in range(ticks)]
-    early = max(chunks - 2, 1)
+    early = max(chunks - 1, 1)
     width = chunks * cols
     rows = n * cap
     side = e // mid
@@ -310,13 +310,18 @@
     def landed_own(t):
         pltpu.make_async_copy(xown.at[t], xown.at[t], own_sem.at[chunks + t - 1]).wait()
 
-    def dispatch(t, c):
-        if t == 0:
-            own_copy(t, c).wait()
+    def dispatch_far(t, c):
         far_copy(t, t, c, s, xown.at[t, c]).start()
+
+    def dispatch_near(t, c):
         pack(xsend.at[t, c], sel[t, side], xown[t, c])
         near(lambda d: x_copy(t, t, c, s, d).start())
         xrecv[t, c, e] = xsend[t, c, e // group - side * sided]
+
+    def dispatch(t, c):
+        own_copy(t, c).wait()
+        dispatch_far(t, c)
+        dispatch_near(t, c)
 
     paired = sections % 2 == 0
     leads = lax.rem(s, 2) == 0
@@ -450,7 +455,7 @@
             def _():
                 landed_own(t + 1)
                 for c in range(chunks):
-                    dispatch(t + 1, c)
+                    dispatch_far(t + 1, c)
 
         if gated[t]:
 
@@ -525,6 +530,11 @@
             def _():
                 for c in range(chunks):
                     relay(t + 1, c)
+
+            @pl.when(jnp.logical_not(has_prev))
+            def _():
+                for c in range(chunks):
+                    dispatch_near(t + 1, c)
 
             @pl.when(held)
             def _():

time: 53.1 us -> 52.5 us (0.989)
  the two profiles are of different devices: /device:TPU:1 before, /device:TPU:2 now
where the time goes in v11:
time: 52.5 us; the launch traced here: 52.3 us
  Pallas kernels  51.6 us (98%)
  local copies, waits for them, and re-layouts  0.73 us (1%)
    pallas_call x1, Pallas kernels, shards(): pl.pallas_call(functools.partial(kernel, n, sections), out_shape=jax.Shap...  51.6 us

profile of v11, /device:TPU:2, one launch (start us, length us, event | category | flops | bytes accessed | tf_op | source)
XLA Modules:
  0.0 52.3 jit_solution(3891755669453736708)
XLA Ops:
  0.0 51.6 %shard_map.82 = bf16[2,32,2560]{2,1,0:T(8,128)(2,1)S(1)} custom-call(bf16[32,2560]{1,0:T(8,128)(2,1)} %bitcast.13, bf16[1,32,2560]{2,1,0:T(8,128)(2,1)} %incoming.1, s32[2,1,2,32]{3,2,1,0:T(2,128)} %bitcast.14, f32[2,1,2,32]{3,2,1,0:T(2,128)} %bitcast.15, f32[1,2560]{1,0:T(1,128)} %gain_hbm.1, bf16[2560,768]{1,0:T(8,128)(2,1)} %bitcast.10, ...), custom_call_target="tpu_custom_call" | custom-call | tf_op jit(solution)/shard_map/pallas_call | solution.py:594
  51.6 0.7 %copy.11 = bf16[2,1,32,2560]{3,2,1,0:T(8,128)(2,1)} copy(bf16[2,1,32,2560]{3,2,1,0:T(8,128)(2,1)S(1)} %bitcast.9) | data formatting | bytes 655360

commit v12 on v11

--- a/solution.py
+++ b/solution.py
@@ -470,10 +470,6 @@
             def _():
                 sent(psend.at[t, :, pl.ds(0, mid)], gate_send.at[t])
 
-            @pl.when(is_gate)
-            def _():
-                sent(fsend.at[t], f_send.at[t])
-
             peers = mid - 1
         else:
             peers = n - 1
@@ -555,6 +551,8 @@
             if mid > 1:
                 for j in range(mid):
                     sent(xrecv.at[t, :, pl.ds(0, mid - 1)], relay_send.at[t, j])
+            if gated[t]:
+                sent(fsend.at[t], f_send.at[t])
 
         if t > 0:
 

time: 52.5 us -> 51.7 us (0.985)
  the two profiles are of different devices: /device:TPU:2 before, /device:TPU:1 now
where the time goes in v12:
time: 51.7 us; the launch traced here: 51.6 us
  Pallas kernels  50.9 us (98%)
  local copies, waits for them, and re-layouts  0.73 us (1%)
    pallas_call x1, Pallas kernels, shards(): pl.pallas_call(functools.partial(kernel, n, sections), out_shape=jax.Shap...  50.9 us

profile of v12, /device:TPU:1, one launch (start us, length us, event | category | flops | bytes accessed | tf_op | source)
XLA Modules:
  0.0 51.6 jit_solution(4772355015585380846)
XLA Ops:
  0.0 50.9 %shard_map.82 = bf16[2,32,2560]{2,1,0:T(8,128)(2,1)S(1)} custom-call(bf16[32,2560]{1,0:T(8,128)(2,1)} %bitcast.13, bf16[1,32,2560]{2,1,0:T(8,128)(2,1)} %incoming.1, s32[2,1,2,32]{3,2,1,0:T(2,128)} %bitcast.14, f32[2,1,2,32]{3,2,1,0:T(2,128)} %bitcast.15, f32[1,2560]{1,0:T(1,128)} %gain_hbm.1, bf16[2560,768]{1,0:T(8,128)(2,1)} %bitcast.10, ...), custom_call_target="tpu_custom_call" | custom-call | tf_op jit(solution)/shard_map/pallas_call | solution.py:592
  50.9 0.7 %copy.11 = bf16[2,1,32,2560]{3,2,1,0:T(8,128)(2,1)} copy(bf16[2,1,32,2560]{3,2,1,0:T(8,128)(2,1)S(1)} %bitcast.9) | data formatting | bytes 655360
